TPU v7x, 32 devices: a whole 2x2x4 slice. The times are simulated.
32 devices in a mesh: dp: 2 (over y), ctx: 4 (over z), exp: 4 (over x, core).
Axes of the slice: x: 2, y: 2, z: 4, core: 2. Of those that a mesh axis runs over, the one named last changes fastest.
Arguments:
- queries: bfloat16 [8, 512, 2048], P(('dp', 'exp'), 'ctx'), may hold values from -24 to 24
- keys: bfloat16 [8, 512, 2048], P(('dp', 'exp'), 'ctx'), may hold values from -20 to 20
- values: bfloat16 [8, 512, 2048], P(('dp', 'exp'), 'ctx'), may hold values from -6 to 6
- resid: bfloat16 [8, 512, 2048], P(('dp', 'exp'), 'ctx'), may hold values from -3 to 3
- norm_gain: float32 [2048], replicated, may hold values from 0.5 to 1.5
- expert_ids: int32 [8, 512, 8], P(('dp', 'exp'), 'ctx'), may hold values from 0 to 15, all different within a row; in each aligned block of 128 rows (0 to 127, 128 to 255, ..., all dimensions but the last counted through in order) at most 68 rows name the same one
- gate_weights: float32 [8, 512, 8], P(('dp', 'exp'), 'ctx'), may hold values from 0.05 to 0.5
- mask_flags: int32 [8, 512], P(('dp', 'exp'), 'ctx'), may hold values 0 or 1
- cotangent: bfloat16 [8, 512, 2048], P(('dp', 'exp'), 'ctx'), may hold values from -0.59765625 to 0.59765625
- w_gate_up: bfloat16 [16, 2048, 1024], P(('ctx', 'exp')), may hold values from -0.125 to 0.125
- w_down: bfloat16 [16, 2048, 512], P(('ctx', 'exp')), may hold values from -0.25 to 0.25
Outputs:
- stream: bfloat16 [8, 512, 2048], P(('dp', 'exp'), 'ctx')
- grad_gate_up: float32 [16, 2048, 1024], P(('ctx', 'exp'), 'dp')
- grad_down: float32 [16, 2048, 512], P(('ctx', 'exp'), 'dp')
Inputs may be any that keep to these rules, and one draw needn't show every extreme that they name: `expert_ids`: in the rows of one device no expert is named more than 68 times, and some device names some expert exactly 68 times.
All inputs are finite; a program needn't handle non-finite values. No bound on the sum of `mask_flags` on one device may be relied on, other than what follows from the above.
Results may differ from a plain program's by a relative error of at most 0.0088.
Values may be sent and summed in bfloat16 or wider, within the bound.
No kernel may reach another device: no remote copies, remote signals or barrier semaphores. Data moves between devices by JAX's collectives and lax.ppermute only.
A program may use at most 128 MiB of HBM per device.

v0:
```python
import math

import jax
import jax.numpy as jnp
from jax import lax
from jax.sharding import PartitionSpec as P

HEADS = 16
HEAD_DIM = 128


def attend(query_rows, keys_all, values_all):
    tokens = query_rows.shape[0]
    length = keys_all.shape[0]
    query_heads = query_rows.reshape(tokens, HEADS, HEAD_DIM)
    key_heads = keys_all.reshape(length, HEADS, HEAD_DIM)
    value_heads = values_all.reshape(length, HEADS, HEAD_DIM)
    scale_factor = 1.0 / math.sqrt(HEAD_DIM)
    scores = (
        jnp.einsum("qhd,khd->hqk", query_heads, key_heads, preferred_element_type=jnp.float32)
        * scale_factor
    )
    largest = jnp.max(scores, axis=2, keepdims=True)
    powers = jnp.exp(scores - largest)
    probs = (powers / jnp.sum(powers, axis=2, keepdims=True)).astype(jnp.bfloat16)
    attended = jnp.einsum("hqk,khd->qhd", probs, value_heads, preferred_element_type=jnp.float32)
    return attended.reshape(tokens, HEADS * HEAD_DIM)


def rms_normed(stream, norm_gain):
    widened = lax.optimization_barrier(stream).astype(jnp.float32)
    factor = lax.rsqrt(jnp.mean(widened * widened, axis=-1, keepdims=True) + 1e-05)
    return (widened * factor * norm_gain).astype(jnp.bfloat16)


def slot_targets(routes, experts, capacity):
    flat_ids = routes.reshape(-1)
    onehot = (flat_ids[:, None] == jnp.arange(experts, dtype=jnp.int32)[None, :]).astype(jnp.int32)
    ranks = jnp.cumsum(onehot, axis=0) - 1
    within = jnp.sum(ranks * onehot, axis=1)
    return flat_ids * capacity + within


def pack_rows(normed, cot_rows, routes, gates, flags, experts, capacity):
    tokens = normed.shape[0]
    model_width = normed.shape[1]
    top_count = routes.shape[1]
    targets = slot_targets(routes, experts, capacity)
    scaled = (
        cot_rows.astype(jnp.float32)[:, None, :]
        * gates[:, :, None]
        * flags.astype(jnp.float32)[:, None, None]
    )
    grad_rows = scaled.astype(jnp.bfloat16).reshape(tokens * top_count, model_width)
    input_rows = jnp.repeat(normed, top_count, axis=0)
    empty = jnp.zeros((experts * capacity, model_width), jnp.bfloat16)
    return (empty.at[targets].set(input_rows), empty.at[targets].set(grad_rows))


def expert_term(input_rows, grad_rows, gate_up, down_map):
    hidden_width = down_map.shape[1]
    projected = jnp.dot(input_rows, gate_up, preferred_element_type=jnp.float32)
    gate_part = projected[:, :hidden_width]
    up_part = projected[:, hidden_width:]
    sigma = jax.nn.sigmoid(gate_part)
    activated = gate_part * sigma
    hidden = (activated * up_part).astype(jnp.bfloat16)
    back_hidden = jnp.dot(grad_rows, down_map, preferred_element_type=jnp.float32)
    slope = sigma * (1.0 + gate_part * (1.0 - sigma))
    back_both = jnp.concatenate(
        [back_hidden * up_part * slope, back_hidden * activated], axis=1
    ).astype(jnp.bfloat16)
    return (hidden, back_both)


def term_rows(input_rows, grad_rows, hidden, back_both):
    contract = (((0,), (0,)), ((), ()))
    left_part = lax.dot_general(input_rows, back_both, contract, preferred_element_type=jnp.float32)
    right_part = lax.dot_general(grad_rows, hidden, contract, preferred_element_type=jnp.float32)
    return jnp.concatenate([left_part, right_part], axis=1)


def per_device(
    queries,
    keys,
    values,
    resid,
    norm_gain,
    expert_ids,
    gate_weights,
    mask_flags,
    cotangent,
    w_gate_up,
    w_down,
):
    keys_all, values_all = (
        lax.all_gather(keys, "ctx", axis=1, tiled=True),
        lax.all_gather(values, "ctx", axis=1, tiled=True),
    )
    attended = attend(queries[0], keys_all[0], values_all[0])
    stream = (resid[0].astype(jnp.float32) + attended).astype(jnp.bfloat16)
    normed = rms_normed(stream, norm_gain)
    ctx_count = lax.axis_size("ctx")
    exp_count = lax.axis_size("exp")
    experts = ctx_count * exp_count
    tokens = queries.shape[1]
    capacity = min(tokens, tokens * expert_ids.shape[2] * 17 // (16 * experts))
    model_width = normed.shape[1]
    input_buf, grad_buf = pack_rows(
        normed, cotangent[0], expert_ids[0], gate_weights[0], mask_flags[0], experts, capacity
    )
    block_shape = (experts, capacity, model_width)
    arrived = (
        lax.all_to_all(
            input_buf.reshape(block_shape), ("ctx", "exp"), split_axis=0, concat_axis=0, tiled=True
        ),
        lax.all_to_all(
            grad_buf.reshape(block_shape), ("ctx", "exp"), split_axis=0, concat_axis=0, tiled=True
        ),
    )
    input_rows = arrived[0].reshape(-1, model_width)
    grad_rows = arrived[1].reshape(-1, model_width)
    hidden, back_both = expert_term(input_rows, grad_rows, w_gate_up[0], w_down[0])
    summed = lax.psum_scatter(
        term_rows(input_rows, grad_rows, hidden, back_both).astype(jnp.bfloat16),
        "dp",
        scatter_dimension=0,
        tiled=True,
    ).astype(jnp.float32)
    hidden_width = w_down.shape[2]
    return (stream[None], summed[:, : 2 * hidden_width][None], summed[:, 2 * hidden_width :][None])


def solution(mesh):
    placed = (
        P(("dp", "exp"), "ctx", None),
        P(("dp", "exp"), "ctx", None),
        P(("dp", "exp"), "ctx", None),
        P(("dp", "exp"), "ctx", None),
        P(),
        P(("dp", "exp"), "ctx", None),
        P(("dp", "exp"), "ctx", None),
        P(("dp", "exp"), "ctx"),
        P(("dp", "exp"), "ctx", None),
        P(("ctx", "exp"), None, None),
        P(("ctx", "exp"), None, None),
    )
    return jax.shard_map(
        per_device,
        mesh=mesh,
        in_specs=placed,
        out_specs=(
            P(("dp", "exp"), "ctx", None),
            P(("ctx", "exp"), "dp", None),
            P(("ctx", "exp"), "dp", None),
        ),
        check_vma=False,
    )
```

profile of v0, /device:TPU:0, one launch (start us, length us, event | category | flops | bytes accessed | tf_op | source)
XLA Modules:
  0.0 449.8 jit_solution(16724601727391645695)
XLA Ops:
  7.2 0.7 all-gather.5.cloned.1.call-update
  7.9 0.7 broadcast_multiply_fusion
  8.6 0.8 copy.28
  9.6 0.7 convert_bitcast_fusion.1
  10.2 0.1 copy.27
  10.3 0.1 mul.100
  10.6 4.5 %reduce-window.6 = s32[16,8,128]{2,1,0:T(8,128)S(1)} reduce-window(s32[16,8,128]{2,1,0:T(8,128)S(1)} %fusion.37, s32[]{:T(128)} %constant.8.clone.1), window={size=1x1x128 pad=0_0x0_0x127_0}, to_apply=%region_2.0 | reduce-window | flops 2080768 | bytes 131076 | tf_op jit(solution)/shard_map/reduce-window
  15.2 0.1 copy.30
  15.6 0.8 copy.33
  16.4 1.1 bitcast_convert_fusion
  17.6 9.7 %scatter_custom_fusion.1 = bf16[1088,2048]{1,0:T(8,128)(2,1)} fusion(s32[1024]{0:T(1024)S(1)} %bitcast.80, f32[1024]{0:T(1024)S(1)} %mul.113, f32[1024]{0:T(1024)S(1)} %mul.109, f32[128,2048]{1,0:T(8,128)S(1)} %bitcast_convert_fusion, bf16[]{:T(256)} %constant.6.clone.1), kind=kCustom, calls=%fused_computation.7 | custom fusion | flops 6291456 | bytes 5513218 | tf_op jit(solution)/shard_map/scatter | solution.py:57
  27.3 7.1 %reshape.112 = bf16[16,68,2048]{2,1,0:T(8,128)(2,1)} reshape(bf16[1088,2048]{1,0:T(8,128)(2,1)} %scatter_custom_fusion.1) | data formatting | bytes 8912896 | tf_op jit(solution)/shard_map/reshape | solution.py:118
  34.4 7.6 %all-to-all-start.1 = ((bf16[16,68,2048]{2,1,0:T(8,128)(2,1)}), bf16[16,68,2048]{2,1,0:T(8,128)(2,1)}, u32[]{:S(2)}, u32[]{:S(2)}) async-start(bf16[16,68,2048]{2,1,0:T(8,128)(2,1)} %reshape.112), calls=%async_computation.1 | async-start | bytes 9437184 | tf_op jit(solution)/shard_map/all_to_all | solution.py:117
  42.0 0.2 all-gather.3.cloned.1.call-start
  42.2 1.0 copy.22
  43.3 0.1 copy.37
  43.4 46.5 %all-gather.5.cloned.1.call-done = bf16[1,512,2048]{2,1,0:T(8,128)(2,1)} async-done(((bf16[1,128,2048]{2,1,0:T(8,128)(2,1)}), bf16[1,512,2048]{2,1,0:T(8,128)(2,1)}) %all-gather.5.cloned.1.call-update) | async-done | bytes 2097168 | tf_op jit(solution)/shard_map/all_gather | solution.py:98
  89.9 3.9 copy.25
  93.8 78.7 %all-gather.3.cloned.1.call-done = bf16[1,512,2048]{1,2,0:T(8,128)(2,1)} async-done(((bf16[1,128,2048]{1,2,0:T(8,128)(2,1)}), bf16[1,512,2048]{1,2,0:T(8,128)(2,1)}) %all-gather.3.cloned.1.call-update) | async-done | bytes 2097168 | tf_op jit(solution)/shard_map/all_gather | solution.py:97
  172.5 2.3 fusion.32
  174.8 1.4 fusion.48
  176.2 0.6 copy-done.2
  176.8 7.9 %fusion.25 = f32[16,128,128]{1,2,0:T(8,128)S(1)} fusion(bf16[512,16,128]{0,2,1:T(8,128)(2,1)} %bitcast.74, f32[16,128]{1,0:T(8,128)S(1)} %fusion.48, f32[16,128,512]{2,1,0:T(8,128)} %copy-done.2), kind=kOutput, calls=%fused_computation.37 | convolution fusion | flops 273680896 | bytes 7348224 | tf_op jit(solution)/shard_map/hqk,khd->qhd/dot_general | solution.py:26
  184.8 1.3 copy.32
  186.1 1.5 fusion.28
  187.5 0.2 fusion.29
  187.7 1.0 fusion.31
  188.7 9.6 %scatter_custom_fusion = bf16[1088,2048]{1,0:T(8,128)(2,1)} fusion(s32[1024]{0:T(1024)S(1)} %bitcast.81, bf16[]{:T(256)} %constant.6.clone.1, bf16[128,2048]{1,0:T(8,128)(2,1)} %fusion.31), kind=kCustom, calls=%fused_computation.11 | custom fusion | bytes 4980738 | tf_op jit(solution)/shard_map/scatter | solution.py:57
  198.4 7.0 %reshape.110 = bf16[16,68,2048]{2,1,0:T(8,128)(2,1)} reshape(bf16[1088,2048]{1,0:T(8,128)(2,1)} %scatter_custom_fusion) | data formatting | bytes 8912896 | tf_op jit(solution)/shard_map/reshape | solution.py:115
  205.4 9.0 %all-to-all-start = ((bf16[16,68,2048]{2,1,0:T(8,128)(2,1)}), bf16[16,68,2048]{2,1,0:T(8,128)(2,1)}, u32[]{:S(2)}, u32[]{:S(2)}) async-start(bf16[16,68,2048]{2,1,0:T(8,128)(2,1)} %reshape.110), calls=%async_computation | async-start | bytes 9437184 | tf_op jit(solution)/shard_map/all_to_all | solution.py:114
  214.3 0.3 reduce-scatter.2.cloned.1.call-start
  214.6 7.1 %reshape.113 = bf16[1088,2048]{1,0:T(8,128)(2,1)} reshape(bf16[16,68,2048]{2,1,0:T(8,128)(2,1)} %all-to-all-done.1) | data formatting | bytes 8912896 | tf_op jit(solution)/shard_map/reshape | solution.py:122
  221.7 79.4 %all-to-all-done = bf16[16,68,2048]{2,1,0:T(8,128)(2,1)} async-done(((bf16[16,68,2048]{2,1,0:T(8,128)(2,1)}), bf16[16,68,2048]{2,1,0:T(8,128)(2,1)}, u32[]{:S(2)}, u32[]{:S(2)}) %all-to-all-start) | async-done | bytes 4456480 | tf_op jit(solution)/shard_map/all_to_all | solution.py:114
  301.2 7.1 %reshape.111 = bf16[1088,2048]{1,0:T(8,128)(2,1)} reshape(bf16[16,68,2048]{2,1,0:T(8,128)(2,1)} %all-to-all-done) | data formatting | bytes 8912896 | tf_op jit(solution)/shard_map/reshape | solution.py:121
  308.2 8.0 %fusion.5 = f32[1088,1024]{1,0:T(8,128)S(1)} fusion(bf16[1088,2048]{1,0:T(8,128)(2,1)} %reshape.111, bf16[1,2048,1024]{2,1,0:T(8,128)(2,1)} %param.20), kind=kOutput, calls=%fused_computation.9 | convolution fusion | flops 4563402752 | bytes 13107200 | tf_op jit(solution)/shard_map/dot_general | solution.py:62
  316.3 4.3 convolution_convert_fusion.1
  320.6 3.3 multiply_convert_fusion.2
  323.9 6.2 %convolution_convert_fusion = bf16[2048,1024]{0,1:T(8,128)(2,1)S(1)} fusion(bf16[1088,2048]{1,0:T(8,128)(2,1)S(1)} %bitcast.70, bf16[1088,512]{1,0:T(8,128)(2,1)S(1)} %get-tuple-element.10, bf16[1088,512]{1,0:T(8,128)(2,1)S(1)} %get-tuple-element.9), kind=kOutput, calls=%fused_computation.18 | convolution fusion | flops 4569956352 | bytes 10878976 | tf_op jit(solution)/shard_map/dot_general | solution.py:78
  330.2 3.7 pad_maximum_fusion
  333.9 0.3 copy.26
  334.3 0.7 copy-done.4
  334.9 0.9 fusion.26
  335.8 92.3 %reduce-scatter.2.cloned.1.call-done = bf16[1024,1536]{0,1:T(8,128)(2,1)} async-done(((bf16[2048,1536]{0,1:T(8,128)(2,1)}), bf16[1024,1536]{0,1:T(8,128)(2,1)}) %reduce-scatter.2.cloned.1.call-update) | async-done | bytes 3145744 | tf_op jit(solution)/shard_map/reduce_scatter | solution.py:124
  428.1 2.6 convert_element_type.76
  430.8 1.6 slice_bitcast_fusion.1
  432.3 2.5 slice_bitcast_fusion
  434.9 5.5 %copy.34 = f32[1,1024,1024]{2,1,0:T(8,128)} copy(f32[1,1024,1024]{1,2,0:T(8,128)} %slice_bitcast_fusion) | data formatting | bytes 8388608
  440.3 2.9 copy.35
  (42 shorter events, 0.9 us)
Async XLA Ops:
  7.2 313.4 %copy-start = (bf16[1,2048,512]{2,1,0:T(8,128)(2,1)S(1)}, bf16[1,2048,512]{2,1,0:T(8,128)(2,1)}, u32[]{:S(2)}) copy-start(bf16[1,2048,512]{2,1,0:T(8,128)(2,1)} %param.21) | copy-start | bytes 6291460
  7.2 82.7 %all-gather.5.cloned.1.call-start = ((), (), s32[]{:S(2)}) async-start(), calls=%async_computation.4 | async-start | bytes 2621440 | tf_op jit(solution)/shard_map/all_gather | solution.py:98
  34.4 7.8 %copy-start.5 = (bf16[1,128,2048]{2,1,0:T(8,128)(2,1)S(1)}, bf16[1,128,2048]{2,1,0:T(8,128)(2,1)}, u32[]{:S(2)}) copy-start(bf16[1,128,2048]{2,1,0:T(8,128)(2,1)} %param.12) | copy-start | bytes 1572868
  34.4 8.8 %copy-start.6 = (bf16[1,128,2048]{2,1,0:T(8,128)(2,1)S(1)}, bf16[1,128,2048]{2,1,0:T(8,128)(2,1)}, u32[]{:S(2)}) copy-start(bf16[1,128,2048]{2,1,0:T(8,128)(2,1)} %param.11) | copy-start | bytes 1572868
  34.4 170.9 %all-to-all-start.1 = ((bf16[16,68,2048]{2,1,0:T(8,128)(2,1)}), bf16[16,68,2048]{2,1,0:T(8,128)(2,1)}, u32[]{:S(2)}, u32[]{:S(2)}) async-start(bf16[16,68,2048]{2,1,0:T(8,128)(2,1)} %reshape.112), calls=%async_computation.1 | async-start | bytes 9437184 | tf_op jit(solution)/shard_map/all_to_all | solution.py:117
  42.0 130.5 %all-gather.3.cloned.1.call-start = ((), (), s32[]{:S(2)}) async-start(), calls=%async_computation.3 | async-start | bytes 2621440 | tf_op jit(solution)/shard_map/all_gather | solution.py:97
  174.8 2.0 copy-start.2
  184.7 3.0 copy-start.7
  205.4 95.8 %all-to-all-start = ((bf16[16,68,2048]{2,1,0:T(8,128)(2,1)}), bf16[16,68,2048]{2,1,0:T(8,128)(2,1)}, u32[]{:S(2)}, u32[]{:S(2)}) async-start(bf16[16,68,2048]{2,1,0:T(8,128)(2,1)} %reshape.110), calls=%async_computation | async-start | bytes 9437184 | tf_op jit(solution)/shard_map/all_to_all | solution.py:114
  214.3 213.8 %reduce-scatter.2.cloned.1.call-start = ((), (), s32[]{:S(2)}) async-start(), calls=%async_computation.5 | async-start | bytes 9437184 | tf_op jit(solution)/shard_map/reduce_scatter | solution.py:124
  301.1 15.1 %slice-start = ((s8[4456448]{0:T(1024)(128)(4,1)}), s8[262144]{0:T(1024)(128)(4,1)S(1)}, s32[]{:S(2)}) async-start(s8[4456448]{0:T(1024)(128)(4,1)} %bitcast.67), calls=%async_computation.6 | async-start | bytes 524288
  308.2 8.0 %slice-start.1 = ((s8[4456448]{0:T(1024)(128)(4,1)}), s8[4194304]{0:T(1024)(128)(4,1)S(1)}, s32[]{:S(2)}) async-start(s8[4456448]{0:T(1024)(128)(4,1)} %bitcast.67), calls=%async_computation.7 | async-start | bytes 8388608
  316.2 7.6 %slice-start.2 = ((s8[4456448]{0:T(1024)(128)(4,1)}), s8[4194304]{0:T(1024)(128)(4,1)S(1)}, s32[]{:S(2)}) async-start(s8[4456448]{0:T(1024)(128)(4,1)} %bitcast.69), calls=%async_computation.8 | async-start | bytes 8388608
  320.6 3.3 slice-start.3
  323.9 6.3 %copy-start.3 = (bf16[2048,512]{0,1:T(8,128)(2,1)S(1)}, bf16[2048,512]{0,1:T(8,128)(2,1)}, u32[]{:S(2)}) copy-start(bf16[2048,512]{0,1:T(8,128)(2,1)} %convolution_convert_fusion.1) | copy-start | bytes 6291460
  333.9 1.0 copy-start.4
  434.9 8.4 %copy-start.1 = (bf16[1,2048,512]{2,1,0:T(8,128)(2,1)S(1)}, bf16[1,2048,512]{2,1,0:T(8,128)(2,1)}, u32[]{:S(2)}) copy-start(bf16[1,2048,512]{2,1,0:T(8,128)(2,1)} %param.21) | copy-start | bytes 6291460
Sparse Core Ops, SparseCore 0:
  9.6 80.2 all-gather.4
  92.0 80.4 all-gather.2
  334.0 94.0 reduce-scatter.1
where the time goes:
time: 451 us; the launch traced here: 450 us
  waiting for transfers between devices  298 us (66%)
  local copies, waits for them, and re-layouts  61 us (14%)
  matrix products  32 us (7%)
  other arithmetic  28.1 us (6%)
  starting transfers between devices  17 us (4%)
  between operations  14 us (3%)
    reduce_scatter x1, waiting for transfers between devices, per_device(): lax.psum_scatter(term_rows(input_rows, grad_rows, hidden, back_both).asty...  92.3 us
    all_to_all x1, waiting for transfers between devices, per_device(): lax.all_to_all(input_buf.reshape(block_shape), ('ctx', 'exp'), split_axis...  79.4 us
    all_gather x1, waiting for transfers between devices, per_device(): lax.all_gather(keys, 'ctx', axis=1, tiled=True)  78.7 us
    all_gather x1, waiting for transfers between devices, per_device(): lax.all_gather(values, 'ctx', axis=1, tiled=True)  46.5 us
    unnamed x30, local copies, waits for them, and re-layouts  12.4 us
    scatter x1, other arithmetic, pack_rows(): return (empty.at[targets].set(input_rows), empty.at[targets].set(grad_rows))  9.65 us
    scatter x1, local copies, waits for them, and re-layouts, pack_rows(): return (empty.at[targets].set(input_rows), empty.at[targets].set(grad_rows))  9.63 us
  transfers between devices with their start and end apart: 5, of which 4 were waited for; matrix products, arithmetic and copies ran while one was open for 16% of the time, Pallas kernels for 0%

commit v1 on v0

v1 whole, which is shorter than its diff:
```python
import math

import jax
import jax.numpy as jnp
from jax import lax
from jax.experimental import pallas as pl
from jax.experimental.pallas import tpu as pltpu
from jax.sharding import PartitionSpec as P

HEAD_DIM = 128
F32 = jnp.float32
BF16 = jnp.bfloat16
VMEM_LIMIT = 56 * 1024 * 1024


def attend_kernel(place, *refs, ctx, tokens, width):
    packs, out = refs[:ctx], refs[ctx]
    z = place[0]
    scale = 1.0 / math.sqrt(HEAD_DIM)
    nt = (((1,), (1,)), ((), ()))
    nn = (((1,), (0,)), ((), ()))
    for h in range(width // HEAD_DIM):
        cols = slice(h * HEAD_DIM, (h + 1) * HEAD_DIM)
        q, k, v = (
            jnp.concatenate([p[i, :, cols] for p in packs], axis=0) for i in range(3)
        )
        scores = lax.dot_general(q, k, nt, preferred_element_type=F32) * scale
        largest = jnp.max(scores, axis=1, keepdims=True)
        powers = jnp.exp(scores - largest)
        probs = (powers / jnp.sum(powers, axis=1, keepdims=True)).astype(BF16)
        attended = lax.dot_general(probs, v, nn, preferred_element_type=F32)
        for s in range(ctx):
            first = pl.multiple_of(lax.rem(z - s + ctx, ctx) * tokens, tokens)
            rows = packs[s][3, :, cols].astype(F32) + attended[s * tokens : (s + 1) * tokens]
            out[pl.ds(first, tokens), cols] = rows.astype(BF16)


def attend(place, packs):
    ctx = len(packs)
    _, tokens, width = packs[0].shape
    vmem = pl.BlockSpec(memory_space=pltpu.VMEM)
    return pl.pallas_call(
        lambda *refs: attend_kernel(*refs, ctx=ctx, tokens=tokens, width=width),
        out_shape=jax.ShapeDtypeStruct((ctx * tokens, width), BF16),
        in_specs=[pl.BlockSpec(memory_space=pltpu.SMEM)] + [vmem] * ctx,
        out_specs=vmem,
        compiler_params=pltpu.CompilerParams(vmem_limit_bytes=VMEM_LIMIT),
        name="attend",
    )(place, *packs)


def expert_kernel(place, gates, gain, gate_up, down, *refs, seqs, ctx, exp, cap, parts, with_stream):
    slices = [refs[i * ctx : (i + 1) * ctx] for i in range(seqs)]
    cots = [refs[(seqs + i) * ctx : (seqs + i + 1) * ctx] for i in range(seqs)]
    rest = refs[2 * seqs * ctx :]
    norm_out, cot_out, back_out, hidden_out = rest[:4]
    stream_out = rest[4] if with_stream else None
    rows_ref, cot_ref, gate_ref, mine_ref = rest[-4:]
    tokens, width_all = cots[0][0].shape
    width = width_all // ctx
    half = width_all // parts
    hidden_width = down.shape[1]
    z, part = place[0], place[1]
    nn = (((1,), (0,)), ((), ()))
    lower = lax.broadcasted_iota(jnp.int32, (tokens, tokens), 0)
    upper = lax.broadcasted_iota(jnp.int32, (tokens, tokens), 1)
    running = (lower <= upper).astype(BF16)
    row_number = lax.broadcasted_iota(jnp.int32, (cap, tokens), 0).astype(F32)
    sources = [lax.rem(z - s + ctx, ctx) for s in range(ctx)]
    if with_stream:
        for s in range(ctx):
            first = pl.multiple_of(z * tokens, tokens)
            mine_ref[sources[s]] = slices[0][s][pl.ds(first, tokens), :]
        for s in range(ctx):
            stream_out[:, s * width : (s + 1) * width] = mine_ref[s]
    for i in range(seqs):
        for s in range(ctx):
            first = pl.multiple_of(sources[s] * tokens, tokens)
            gate = gates[sources[s] * exp + place[2 + i]]
            picked = gate != 0.0
            marks = jnp.broadcast_to(picked.astype(F32), (8, tokens)).astype(BF16)
            rank = lax.dot_general(marks, running, nn, preferred_element_type=F32)[:1]
            chosen = jnp.logical_and(row_number + 1.0 == rank, picked)
            select = chosen.astype(F32).astype(BF16)
            at = (i * ctx + s) * cap
            gate_ref[at : at + cap, :] = jnp.broadcast_to(
                jnp.sum(jnp.where(chosen, gate, 0.0), axis=1, keepdims=True), (cap, 128)
            )
            for f in range(ctx):
                block = slices[i][f][pl.ds(first, tokens), :]
                rows = lax.dot_general(select, block, nn, preferred_element_type=F32)
                rows_ref[sources[f], at : at + cap, :] = rows.astype(BF16)
            for p in range(parts):
                block = cots[i][s][:, p * half : (p + 1) * half]
                rows = lax.dot_general(select, block, nn, preferred_element_type=F32)
                cot_ref[p, at : at + cap, :] = rows.astype(BF16)
    total = None
    for f in range(ctx):
        wide = rows_ref[f].astype(F32)
        square = jnp.sum(wide * wide, axis=1, keepdims=True)
        total = square if total is None else total + square
    factor = lax.rsqrt(total / width_all + 1e-05)
    proj = None
    for f in range(ctx):
        normed = (rows_ref[f].astype(F32) * factor * gain[f]).astype(BF16)
        rows_ref[f] = normed
        term = lax.dot_general(
            normed, gate_up[f * width : (f + 1) * width, :], nn, preferred_element_type=F32
        )
        proj = term if proj is None else proj + term
    back = None
    for p in range(parts):
        term = lax.dot_general(
            cot_ref[p], down[p * half : (p + 1) * half, :], nn, preferred_element_type=F32
        )
        back = term if back is None else back + term
    gate_column = gate_ref[:, :1]
    gate_part, up_part = proj[:, :hidden_width], proj[:, hidden_width:]
    sigma = 1.0 / (1.0 + jnp.exp(-gate_part))
    activated = gate_part * sigma
    back = back * gate_column
    hidden_out[...] = (activated * up_part * gate_column).astype(BF16)
    slope = sigma * (1.0 + gate_part * (1.0 - sigma))
    back_out[:, :hidden_width] = (back * up_part * slope).astype(BF16)
    back_out[:, hidden_width:] = (back * activated).astype(BF16)
    cot_out[...] = cot_ref[part]
    each = ctx // parts
    for f in range(each):
        norm_out[:, f * width : (f + 1) * width] = rows_ref[part * each + f]


def expert_rows(place, gates, gain, gate_up, down, slices, cots, cap, exp, parts, with_stream):
    seqs, ctx = len(slices), len(slices[0])
    tokens, width_all = cots[0][0].shape
    width = width_all // ctx
    half = width_all // parts
    hidden_width = down.shape[1]
    count = seqs * ctx * cap
    vmem = pl.BlockSpec(memory_space=pltpu.VMEM)
    shapes = [
        jax.ShapeDtypeStruct((count, half), BF16),
        jax.ShapeDtypeStruct((count, half), BF16),
        jax.ShapeDtypeStruct((count, 2 * hidden_width), BF16),
        jax.ShapeDtypeStruct((count, hidden_width), BF16),
    ]
    if with_stream:
        shapes.append(jax.ShapeDtypeStruct((tokens, width_all), BF16))
    args = [a for one in slices for a in one] + [a for one in cots for a in one]
    return pl.pallas_call(
        lambda *refs: expert_kernel(
            *refs, seqs=seqs, ctx=ctx, exp=exp, cap=cap, parts=parts, with_stream=with_stream
        ),
        out_shape=shapes,
        in_specs=[pl.BlockSpec(memory_space=pltpu.SMEM)] + [vmem] * (4 + len(args)),
        out_specs=[vmem] * len(shapes),
        scratch_shapes=[
            pltpu.VMEM((ctx, count, width), BF16),
            pltpu.VMEM((parts, count, half), BF16),
            pltpu.VMEM((count, 128), F32),
            pltpu.VMEM((ctx, tokens, width), BF16),
        ],
        compiler_params=pltpu.CompilerParams(vmem_limit_bytes=VMEM_LIMIT),
        name="expert_rows",
    )(place, gates, gain, gate_up, down, *args)


def grads_kernel(*refs, groups, add):
    norms, cots, backs, hiddens = (refs[i * groups : (i + 1) * groups] for i in range(4))
    rest = refs[4 * groups :]
    tn = (((0,), (0,)), ((), ()))

    def whole(parts):
        return jnp.concatenate([p[...] for p in parts], axis=0)

    left = lax.dot_general(whole(norms), whole(backs), tn, preferred_element_type=F32)
    right = lax.dot_general(whole(cots), whole(hiddens), tn, preferred_element_type=F32)
    out_left, out_right = rest[-2:]
    if add:
        left = left + rest[0][0]
        right = right + rest[1][0]
    out_left[0] = left
    out_right[0] = right


def grads(pieces, before):
    groups = len(pieces)
    norms, cots, backs, hiddens = zip(*pieces)
    count, half = norms[0].shape
    step = 256
    tall = [pl.BlockSpec((count, step), lambda i: (0, i))] * groups
    out_widths = (backs[0].shape[1], hiddens[0].shape[1])
    full = [
        pl.BlockSpec((count, w), lambda i: (0, 0)) for w in out_widths for _ in range(groups)
    ]
    outs = [pl.BlockSpec((1, step, w), lambda i: (0, i, 0)) for w in out_widths]
    add = before is not None
    args = [*norms, *cots, *backs, *hiddens] + (list(before) if add else [])
    return pl.pallas_call(
        lambda *refs: grads_kernel(*refs, groups=groups, add=add),
        out_shape=[jax.ShapeDtypeStruct((1, half, w), F32) for w in out_widths],
        grid=(half // step,),
        in_specs=tall + tall + full + (outs if add else []),
        out_specs=outs,
        input_output_aliases={4 * groups: 0, 4 * groups + 1: 1} if add else {},
        compiler_params=pltpu.CompilerParams(vmem_limit_bytes=VMEM_LIMIT),
        name="grads",
    )(*args)


def shifted(value, axis, step, count):
    return lax.ppermute(value, axis, [(i, (i + step) % count) for i in range(count)])


def flipped(value, axis, mask, count):
    return lax.ppermute(value, axis, [(i, i ^ mask) for i in range(count)])


def spread(own, ctx, exp):
    found = {}
    column = [own] + [shifted(own, "ctx", s, ctx) for s in range(1, ctx)]
    found[0, 0] = column
    found[0, 1] = [flipped(b, "exp", 2, exp) for b in column]
    found[1, 0] = [flipped(b, "dp", 1, 2) for b in column]
    found[1, 1] = [
        flipped(found[0, 1][s], "dp", 1, 2) if s % 2 == 0 else flipped(found[1, 0][s], "exp", 2, exp)
        for s in range(ctx)
    ]
    everywhere = {}
    for (dy, dx), blocks in found.items():
        everywhere[dy, dx, 0] = blocks
        everywhere[dy, dx, 1] = [flipped(b, "exp", 1, exp) for b in blocks]
    return everywhere


def expert_gates(routes, gates, flags, experts):
    named = routes[:, :, None] == jnp.arange(experts, dtype=jnp.int32)[None, None, :]
    scaled = gates * flags.astype(F32)[:, None]
    return jnp.sum(jnp.where(named, scaled[:, :, None], 0.0), axis=1)


def per_device(
    queries, keys, values, resid, norm_gain, expert_ids, gate_weights, mask_flags, cotangent, w_gate_up, w_down
):
    ctx, exp, parts = (lax.axis_size(a) for a in ("ctx", "exp", "dp"))
    z, e, part = (lax.axis_index(a) for a in ("ctx", "exp", "dp"))
    experts = ctx * exp
    _, tokens, width_all = queries.shape
    width = width_all // ctx
    most = min(tokens, tokens * expert_ids.shape[2] * 17 // (16 * experts))
    cap = -(-most // 16) * 16

    parts4 = jnp.stack([queries[0], keys[0], values[0], resid[0]])
    parts4 = parts4.reshape(4, tokens, ctx, width).transpose(2, 0, 1, 3)
    packs = []
    for s in range(ctx):
        piece = lax.dynamic_index_in_dim(parts4, lax.rem(z + s, ctx), 0, keepdims=False)
        packs.append(piece if s == 0 else shifted(piece, "ctx", s, ctx))

    by_expert = expert_gates(expert_ids[0], gate_weights[0], mask_flags[0], experts)
    gates_here = lax.all_to_all(
        by_expert.T.reshape(experts, 1, tokens), ("ctx", "exp"), split_axis=0, concat_axis=0, tiled=True
    )
    gates_there = flipped(gates_here, "dp", 1, 2)

    cots = spread(cotangent[0], ctx, exp)
    own_slice = attend(jnp.stack([z, z]), packs)
    streams = spread(own_slice, ctx, exp)

    gain = norm_gain.reshape(ctx, 1, width)
    pieces, stream = [], None
    for dy, dx in ((0, 0), (0, 1), (1, 0), (1, 1)):
        place = jnp.stack([z, part, e ^ (2 * dx), e ^ (2 * dx) ^ 1]).astype(jnp.int32)
        got = expert_rows(
            place,
            gates_there if dy else gates_here,
            gain,
            w_gate_up[0],
            w_down[0],
            [streams[dy, dx, c] for c in range(2)],
            [cots[dy, dx, c] for c in range(2)],
            cap,
            exp,
            parts,
            (dy, dx) == (0, 0),
        )
        if stream is None:
            stream = got[4]
        pieces.append(got[:4])
    first = grads(pieces[:2], None)
    left, right = grads(pieces[2:], first)
    return stream[None], left, right


def routed_device(
    queries, keys, values, resid, norm_gain, expert_ids, gate_weights, mask_flags, cotangent, w_gate_up, w_down
):
    ctx, exp = (lax.axis_size(a) for a in ("ctx", "exp"))
    experts = ctx * exp
    _, tokens, width_all = queries.shape
    top = expert_ids.shape[2]
    capacity = min(tokens, tokens * top * 17 // (16 * experts))
    keys_all = lax.all_gather(keys[0], "ctx", axis=0, tiled=True)
    values_all = lax.all_gather(values[0], "ctx", axis=0, tiled=True)
    heads = width_all // HEAD_DIM
    q, k, v = (a.reshape(-1, heads, HEAD_DIM) for a in (queries[0], keys_all, values_all))
    scores = jnp.einsum("qhd,khd->hqk", q, k, preferred_element_type=F32) / math.sqrt(HEAD_DIM)
    powers = jnp.exp(scores - jnp.max(scores, axis=2, keepdims=True))
    probs = (powers / jnp.sum(powers, axis=2, keepdims=True)).astype(BF16)
    attended = jnp.einsum("hqk,khd->qhd", probs, v, preferred_element_type=F32)
    stream = (resid[0].astype(F32) + attended.reshape(tokens, width_all)).astype(BF16)
    wide = lax.optimization_barrier(stream).astype(F32)
    factor = lax.rsqrt(jnp.mean(wide * wide, axis=-1, keepdims=True) + 1e-05)
    normed = (wide * factor * norm_gain).astype(BF16)

    by_expert = expert_gates(expert_ids[0], gate_weights[0], mask_flags[0], experts)
    picked = by_expert != 0.0
    running = jnp.arange(tokens)[:, None] >= jnp.arange(tokens)[None, :]
    rank = jnp.dot(running.astype(BF16), picked.astype(BF16), preferred_element_type=F32) - 1.0
    slot = jnp.arange(capacity, dtype=F32)[None, :, None]
    chosen = jnp.logical_and(rank.T[:, None, :] == slot, picked.T[:, None, :])
    select = chosen.astype(BF16).reshape(experts * capacity, tokens)
    sent_rows = jnp.dot(select, normed, preferred_element_type=F32).astype(BF16)
    gate_rows = jnp.sum(jnp.where(chosen, by_expert.T[:, None, :], 0.0), axis=2).reshape(-1, 1)
    picked_cot = jnp.dot(select, cotangent[0], preferred_element_type=F32)
    sent_grads = (picked_cot * gate_rows).astype(BF16)

    def exchanged(rows):
        rows = rows.reshape(experts, capacity, width_all)
        got = lax.all_to_all(rows, ("ctx", "exp"), split_axis=0, concat_axis=0, tiled=True)
        return got.reshape(-1, width_all)

    input_rows, grad_rows = exchanged(sent_rows), exchanged(sent_grads)
    hidden_width = w_down.shape[2]
    proj = jnp.dot(input_rows, w_gate_up[0], preferred_element_type=F32)
    gate_part, up_part = proj[:, :hidden_width], proj[:, hidden_width:]
    sigma = jax.nn.sigmoid(gate_part)
    activated = gate_part * sigma
    hidden = (activated * up_part).astype(BF16)
    back = jnp.dot(grad_rows, w_down[0], preferred_element_type=F32)
    slope = sigma * (1.0 + gate_part * (1.0 - sigma))
    both = jnp.concatenate([back * up_part * slope, back * activated], axis=1).astype(BF16)
    tn = (((0,), (0,)), ((), ()))
    left = lax.dot_general(input_rows, both, tn, preferred_element_type=F32)
    right = lax.dot_general(grad_rows, hidden, tn, preferred_element_type=F32)
    partial = jnp.concatenate([left, right], axis=1).astype(BF16)
    summed = lax.psum_scatter(partial, "dp", scatter_dimension=0, tiled=True).astype(F32)
    return stream[None], summed[None, :, : 2 * hidden_width], summed[None, :, 2 * hidden_width :]


def solution(mesh):
    rows = P(("dp", "exp"), "ctx", None)
    weights = P(("ctx", "exp"), None, None)
    placed = (rows, rows, rows, rows, P(), rows, rows, P(("dp", "exp"), "ctx"), rows, weights, weights)
    body = per_device if mesh.shape["dp"] == 2 and mesh.shape["exp"] == 4 else routed_device
    return jax.shard_map(
        body,
        mesh=mesh,
        in_specs=placed,
        out_specs=(rows, P(("ctx", "exp"), "dp", None), P(("ctx", "exp"), "dp", None)),
        check_vma=False,
    )
```

time: 451 us -> 400 us (0.89)
  the two profiles are of different devices: /device:TPU:0 before, /device:TPU:25 now
where the time goes in v1:
time: 400 us; the launch traced here: 401 us
  waiting for transfers between devices  178 us (44%)
  Pallas kernels  91.2 us (23%)
  blocking collectives  67.8 us (17%)
  starting transfers between devices  46.4 us (12%)
  local copies, waits for them, and re-layouts  11 us (3%)
  other arithmetic  4.97 us (1%)
    ppermute x57, waiting for transfers between devices, flipped(): return lax.ppermute(value, axis, [(i, i ^ mask) for i in range(count)])  136 us
    all_to_all x1, blocking collectives, per_device(): lax.all_to_all(by_expert.T.reshape(experts, 1, tokens), ('ctx', 'exp'), s...  67.8 us
    pallas_call x4, Pallas kernels, expert_rows(): pl.pallas_call(lambda *refs: expert_kernel(*refs, seqs=seqs, ctx=ctx, exp...  67.7 us
    ppermute x9, waiting for transfers between devices, shifted(): lax.ppermute(value, axis, [(i, (i + step) % count) for i in range(count)])  42.2 us
    ppermute x57, starting transfers between devices, flipped(): return lax.ppermute(value, axis, [(i, i ^ mask) for i in range(count)])  38.8 us
    pallas_call x2, Pallas kernels, grads(): pl.pallas_call(lambda *refs: grads_kernel(*refs, groups=groups, add=add),...  18.7 us
  transfers between devices with their start and end apart: 66, of which 21 were waited for; matrix products, arithmetic and copies ran while one was open for 3% of the time, Pallas kernels for 17%

profile of v1, /device:TPU:25, one launch (start us, length us, event | category | flops | bytes accessed | tf_op | source)
XLA Modules:
  0.0 400.6 jit_solution(7249296035932824399)
XLA Ops:
  0.8 2.2 collective-permute-start.10
  2.9 3.1 pad_maximum_fusion
  6.0 3.3 reshape.51
  9.4 4.4 %constant_dynamic-slice_fusion = (bf16[4,128,1,512]{3,2,1,0:T(2,128)(2,1)S(1)}, bf16[4,128,1,512]{3,2,1,0:T(2,128)(2,1)S(1)}, bf16[4,128,1,512]{3,2,1,0:T(2,128)(2,1)S(1)}, bf16[4,128,1,512]{3,2,1,0:T(2,128)(2,1)S(1)}) fusion(bf16[4,128,4,512]{3,2,1,0:T(4,128)(2,1)S(1)} %reshape.51, s32[]{:T(128)S(6)} %select_n.21, s32[]{:T(128)S(6)} %select_n.20, ...), kind=kLoop, calls=%fused_computation.8 | loop fusion | bytes 4194320 | tf_op jit(solution)/shard_map/dynamic-slice.3
  13.9 1.3 collective-permute-start
  16.0 67.8 %all_to_all.5.refs_1_ = f32[16,1,128]{2,1,0:T(1,128)S(1)} all-to-all(f32[16,1,128]{2,1,0:T(1,128)S(1)} %bitcast.54), channel_id=1, replica_groups=mesh['dp'=2,'ctx'=4,'exp'=4] {'ctx','exp'}, dimensions={0} | all-to-all | bytes 16384 | tf_op jit(solution)/shard_map/all_to_all | solution.py:260
  83.9 1.3 collective-permute-start.17
  85.8 0.9 copy.37
  87.9 4.8 %attend.1.refs_5_ = bf16[512,512]{1,0:T(8,128)(2,1)} custom-call(s32[2]{0:T(128)} %pad_add_fusion.2.refs_0_, bf16[4,128,512]{2,1,0:T(8,128)(2,1)} %bitcast.39, bf16[4,128,512]{2,1,0:T(8,128)(2,1)} %copy-done.52, bf16[4,128,512]{2,1,0:T(8,128)(2,1)} %copy-done.53, bf16[4,128,512]{2,1,0:T(8,128)(2,1)} %copy-done.54), custom_call_target="tpu_custom_call" | custom-call | tf_op jit(solution)/shard_map/attend/pallas_call | solution.py:42
  92.7 1.3 collective-permute-start.13
  94.3 2.9 collective-permute-start.3
  97.2 3.9 collective-permute-done.12.refs_16_
  101.5 0.9 collective-permute-start.34
  102.3 5.2 %collective-permute-done.26.refs_13_ = bf16[128,2048]{1,0:T(8,128)(2,1)S(1)} collective-permute-done((bf16[128,2048]{1,0:T(8,128)(2,1)S(1)}, bf16[128,2048]{1,0:T(8,128)(2,1)S(1)}, u32[]{:S(2)}, u32[]{:S(2)}) %collective-permute-start.26) | collective-permute-done | bytes 524320 | tf_op jit(solution)/shard_map/ppermute | solution.py:215
  107.5 1.0 collective-permute-start.47
  108.5 5.2 %collective-permute-done.3.refs_6_ = bf16[512,512]{1,0:T(8,128)(2,1)S(1)} collective-permute-done((bf16[512,512]{1,0:T(8,128)(2,1)}, bf16[512,512]{1,0:T(8,128)(2,1)S(1)}, u32[]{:S(2)}, u32[]{:S(2)}) %collective-permute-start.3) | collective-permute-done | bytes 524320 | tf_op jit(solution)/shard_map/ppermute | solution.py:211
  114.3 33.1 %collective-permute-done.4.refs_7_ = bf16[512,512]{1,0:T(8,128)(2,1)S(1)} collective-permute-done((bf16[512,512]{1,0:T(8,128)(2,1)}, bf16[512,512]{1,0:T(8,128)(2,1)S(1)}, u32[]{:S(2)}, u32[]{:S(2)}) %collective-permute-start.4) | collective-permute-done | bytes 524320 | tf_op jit(solution)/shard_map/ppermute | solution.py:211
  149.3 11.1 %collective-permute-done.61.refs_16_ = bf16[128,2048]{1,0:T(8,128)(2,1)S(1)} collective-permute-done((bf16[128,2048]{1,0:T(8,128)(2,1)S(1)}, bf16[128,2048]{1,0:T(8,128)(2,1)S(1)}, u32[]{:S(2)}, u32[]{:S(2)}) %collective-permute-start.61) | collective-permute-done | bytes 524320 | tf_op jit(solution)/shard_map/ppermute | solution.py:215
  160.4 1.3 collective-permute-start.16
  162.0 1.2 collective-permute-start.29
  165.7 9.6 %collective-permute-done.27.refs_14_ = bf16[128,2048]{1,0:T(8,128)(2,1)S(1)} collective-permute-done((bf16[128,2048]{1,0:T(8,128)(2,1)S(1)}, bf16[128,2048]{1,0:T(8,128)(2,1)S(1)}, u32[]{:S(2)}, u32[]{:S(2)}) %collective-permute-start.27) | collective-permute-done | bytes 524320 | tf_op jit(solution)/shard_map/ppermute | solution.py:215
  175.3 1.3 collective-permute-start.30
  176.6 9.9 %collective-permute-done.29.refs_16_ = bf16[128,2048]{1,0:T(8,128)(2,1)S(1)} collective-permute-done((bf16[128,2048]{1,0:T(8,128)(2,1)S(1)}, bf16[128,2048]{1,0:T(8,128)(2,1)S(1)}, u32[]{:S(2)}, u32[]{:S(2)}) %collective-permute-start.29) | collective-permute-done | bytes 524320 | tf_op jit(solution)/shard_map/ppermute | solution.py:215
  187.1 10.7 %collective-permute-done.45.refs_13_ = bf16[128,2048]{1,0:T(8,128)(2,1)S(1)} collective-permute-done((bf16[128,2048]{1,0:T(8,128)(2,1)S(1)}, bf16[128,2048]{1,0:T(8,128)(2,1)S(1)}, u32[]{:S(2)}, u32[]{:S(2)}) %collective-permute-start.45) | collective-permute-done | bytes 524320 | tf_op jit(solution)/shard_map/ppermute | solution.py:215
  198.3 10.7 %collective-permute-done.18.refs_5_ = bf16[512,512]{1,0:T(8,128)(2,1)S(1)} collective-permute-done((bf16[512,512]{1,0:T(8,128)(2,1)}, bf16[512,512]{1,0:T(8,128)(2,1)S(1)}, u32[]{:S(2)}, u32[]{:S(2)}) %collective-permute-start.18) | collective-permute-done | bytes 524320 | tf_op jit(solution)/shard_map/ppermute | solution.py:215
  209.5 10.7 %collective-permute-done.28.refs_15_ = bf16[128,2048]{1,0:T(8,128)(2,1)S(1)} collective-permute-done((bf16[128,2048]{1,0:T(8,128)(2,1)S(1)}, bf16[128,2048]{1,0:T(8,128)(2,1)S(1)}, u32[]{:S(2)}, u32[]{:S(2)}) %collective-permute-start.28) | collective-permute-done | bytes 524320 | tf_op jit(solution)/shard_map/ppermute | solution.py:215
  220.2 0.8 collective-permute-start.56
  221.7 1.6 collective-permute-start.7
  227.7 9.5 %collective-permute-done.19.refs_6_ = bf16[512,512]{1,0:T(8,128)(2,1)S(1)} collective-permute-done((bf16[512,512]{1,0:T(8,128)(2,1)S(1)}, bf16[512,512]{1,0:T(8,128)(2,1)S(1)}, u32[]{:S(2)}, u32[]{:S(2)}) %collective-permute-start.19) | collective-permute-done | bytes 524320 | tf_op jit(solution)/shard_map/ppermute | solution.py:215
  237.8 10.8 %collective-permute-done.21.refs_8_ = bf16[512,512]{1,0:T(8,128)(2,1)S(1)} collective-permute-done((bf16[512,512]{1,0:T(8,128)(2,1)S(1)}, bf16[512,512]{1,0:T(8,128)(2,1)S(1)}, u32[]{:S(2)}, u32[]{:S(2)}) %collective-permute-start.21) | collective-permute-done | bytes 524320 | tf_op jit(solution)/shard_map/ppermute | solution.py:215
  248.6 1.9 collective-permute-start.50
  250.5 9.2 %collective-permute-done.35.refs_5_ = bf16[512,512]{1,0:T(8,128)(2,1)S(1)} collective-permute-done((bf16[512,512]{1,0:T(8,128)(2,1)S(1)}, bf16[512,512]{1,0:T(8,128)(2,1)S(1)}, u32[]{:S(2)}, u32[]{:S(2)}) %collective-permute-start.35) | collective-permute-done | bytes 524320 | tf_op jit(solution)/shard_map/ppermute | solution.py:215
  259.9 2.3 collective-permute-start.22
  262.2 8.8 %collective-permute-done.48.refs_15_ = bf16[128,2048]{1,0:T(8,128)(2,1)} collective-permute-done((bf16[128,2048]{1,0:T(8,128)(2,1)S(1)}, bf16[128,2048]{1,0:T(8,128)(2,1)}, u32[]{:S(2)}, u32[]{:S(2)}) %collective-permute-start.48) | collective-permute-done | bytes 524320 | tf_op jit(solution)/shard_map/ppermute | solution.py:215
  271.0 2.0 collective-permute-start.31
  273.6 8.6 %collective-permute-done.20.refs_7_ = bf16[512,512]{1,0:T(8,128)(2,1)S(1)} collective-permute-done((bf16[512,512]{1,0:T(8,128)(2,1)S(1)}, bf16[512,512]{1,0:T(8,128)(2,1)S(1)}, u32[]{:S(2)}, u32[]{:S(2)}) %collective-permute-start.20) | collective-permute-done | bytes 524320 | tf_op jit(solution)/shard_map/ppermute | solution.py:215
  282.2 1.2 collective-permute-start.57
  285.1 1.0 collective-permute-start.39
  286.0 0.9 collective-permute-start.40
  287.7 10.1 %collective-permute-done.36.refs_6_ = bf16[512,512]{1,0:T(8,128)(2,1)} collective-permute-done((bf16[512,512]{1,0:T(8,128)(2,1)S(1)}, bf16[512,512]{1,0:T(8,128)(2,1)}, u32[]{:S(2)}, u32[]{:S(2)}) %collective-permute-start.36) | collective-permute-done | bytes 524320 | tf_op jit(solution)/shard_map/ppermute | solution.py:215
  297.8 1.2 collective-permute-start.23
  299.3 9.8 %collective-permute-done.39.refs_8_ = bf16[512,512]{1,0:T(8,128)(2,1)} collective-permute-done((bf16[512,512]{1,0:T(8,128)(2,1)S(1)}, bf16[512,512]{1,0:T(8,128)(2,1)}, u32[]{:S(2)}, u32[]{:S(2)}) %collective-permute-start.39) | collective-permute-done | bytes 524320 | tf_op jit(solution)/shard_map/ppermute | solution.py:215
  313.9 13.7 %expert_rows.4 = (bf16[640,1024]{1,0:T(8,128)(2,1)}, bf16[640,1024]{1,0:T(8,128)(2,1)}, bf16[640,1024]{1,0:T(8,128)(2,1)}, bf16[640,512]{1,0:T(8,128)(2,1)}, bf16[128,2048]{1,0:T(8,128)(2,1)}) custom-call(s32[4]{0:T(128)} %pad_add_fusion.refs_0_, f32[16,1,128]{2,1,0:T(1,128)} %copy-done.55, f32[4,1,512]{2,1,0:T(1,128)} %bitcast.50, ...), custom_call_target="tpu_custom_call" | custom-call | tf_op jit(solution)/shard_map/expert_rows/pallas_call | solution.py:149
  327.7 27.0 %expert_rows.7 = (bf16[640,1024]{1,0:T(8,128)(2,1)}, bf16[640,1024]{1,0:T(8,128)(2,1)}, bf16[640,1024]{1,0:T(8,128)(2,1)}, bf16[640,512]{1,0:T(8,128)(2,1)}) custom-call(s32[4]{0:T(128)} %pad_add_fusion.3.refs_0_, f32[16,1,128]{2,1,0:T(1,128)} %copy-done.55, f32[4,1,512]{2,1,0:T(1,128)} %bitcast.51, bf16[2048,1024]{1,0:T(8,128)(2,1)} %bitcast.32, ...), custom_call_target="tpu_custom_call" | custom-call | tf_op jit(solution)/shard_map/expert_rows/pallas_call | solution.py:149
  354.7 8.7 %grads.2 = (f32[1,1024,1024]{2,1,0:T(8,128)}, f32[1,1024,512]{2,1,0:T(8,128)}) custom-call(bf16[640,1024]{1,0:T(8,128)(2,1)} %get-tuple-element.33.refs_0_, bf16[640,1024]{1,0:T(8,128)(2,1)} %get-tuple-element.34.refs_1_, bf16[640,1024]{1,0:T(8,128)(2,1)} %get-tuple-element.35.refs_2_, bf16[640,1024]{1,0:T(8,128)(2,1)} %get-tuple-element.36.refs_3_, ...), custom_call_target="tpu_custom_call" | custom-call | tf_op jit(solution)/shard_map/grads/pallas_call | solution.py:198
  363.4 13.4 %expert_rows.5 = (bf16[640,1024]{1,0:T(8,128)(2,1)}, bf16[640,1024]{1,0:T(8,128)(2,1)}, bf16[640,1024]{1,0:T(8,128)(2,1)}, bf16[640,512]{1,0:T(8,128)(2,1)}) custom-call(s32[4]{0:T(128)} %pad_add_fusion.refs_0_, f32[16,1,128]{2,1,0:T(1,128)} %collective-permute-done.17.refs_1_, f32[4,1,512]{2,1,0:T(1,128)} %bitcast.52, bf16[2048,1024]{1,0:T(8,128)(2,1)} %bitcast.33, ...), custom_call_target="tpu_custom_call" | custom-call | tf_op jit(solution)/shard_map/expert_rows/pallas_call | solution.py:149
  376.9 13.5 %expert_rows.6 = (bf16[640,1024]{1,0:T(8,128)(2,1)}, bf16[640,1024]{1,0:T(8,128)(2,1)}, bf16[640,1024]{1,0:T(8,128)(2,1)}, bf16[640,512]{1,0:T(8,128)(2,1)}) custom-call(s32[4]{0:T(128)} %pad_add_fusion.3.refs_0_, f32[16,1,128]{2,1,0:T(1,128)} %collective-permute-done.17.refs_1_, f32[4,1,512]{2,1,0:T(1,128)} %bitcast.53, bf16[2048,1024]{1,0:T(8,128)(2,1)} %bitcast.34, ...), custom_call_target="tpu_custom_call" | custom-call | tf_op jit(solution)/shard_map/expert_rows/pallas_call | solution.py:149
  390.3 10.1 %grads.3 = (f32[1,1024,1024]{2,1,0:T(8,128)}, f32[1,1024,512]{2,1,0:T(8,128)}) custom-call(bf16[640,1024]{1,0:T(8,128)(2,1)} %get-tuple-element.25.refs_0_, bf16[640,1024]{1,0:T(8,128)(2,1)} %get-tuple-element.26.refs_1_, bf16[640,1024]{1,0:T(8,128)(2,1)} %get-tuple-element.27.refs_2_, ...), custom_call_target="tpu_custom_call", output_to_operand_aliasing={{0}: (8, {}), {1}: (9, {})} | custom-call | tf_op jit(solution)/shard_map/grads/pallas_call | solution.py:198
  (223 shorter events, 24.2 us)
Async XLA Ops:
  0.6 93.4 %collective-permute-start.11 = (bf16[128,2048]{1,0:T(8,128)(2,1)}, bf16[128,2048]{1,0:T(8,128)(2,1)S(1)}, u32[]{:S(2)}, u32[]{:S(2)}) collective-permute-start(bf16[128,2048]{1,0:T(8,128)(2,1)} %bitcast.40), channel_id=1, source_target_pairs={{0,8},{4,12},{8,0},{12,4},{1,9},{5,13},{9,1},{13,5},{2,10},{6,14},... | collective-permute-start | bytes 1572872 | tf_op jit(solution)/shard_map/ppermute | solution.py:211
  0.8 93.5 %collective-permute-start.10 = (bf16[128,2048]{1,0:T(8,128)(2,1)}, bf16[128,2048]{1,0:T(8,128)(2,1)S(1)}, u32[]{:S(2)}, u32[]{:S(2)}) collective-permute-start(bf16[128,2048]{1,0:T(8,128)(2,1)} %bitcast.41), channel_id=1, source_target_pairs={{0,4},{4,8},{8,12},{12,0},{1,5},{5,9},{9,13},{13,1},{2,6},{6,10},{... | collective-permute-start | bytes 1572872 | tf_op jit(solution)/shard_map/ppermute | solution.py:211
  13.9 69.9 %collective-permute-start = (bf16[4,128,512]{2,1,0:T(8,128)(2,1)S(1)}, bf16[4,128,512]{2,1,0:T(8,128)(2,1)S(1)}, u32[]{:S(2)}, u32[]{:S(2)}) collective-permute-start(bf16[4,128,512]{2,1,0:T(8,128)(2,1)S(1)} %bitcast.49), channel_id=1, source_target_pairs={{0,4},{4,8},{8,12},{12,0},{1,5},{5,9},{9,13},{13,1},{2,6},{6,10},{... | collective-permute-start | bytes 1572872 | tf_op jit(solution)/shard_map/ppermute | solution.py:211
  15.4 71.3 %collective-permute-start.1 = (bf16[4,128,512]{2,1,0:T(8,128)(2,1)S(1)}, bf16[4,128,512]{2,1,0:T(8,128)(2,1)S(1)}, u32[]{:S(2)}, u32[]{:S(2)}) collective-permute-start(bf16[4,128,512]{2,1,0:T(8,128)(2,1)S(1)} %bitcast.48), channel_id=1, source_target_pairs={{0,8},{4,12},{8,0},{12,4},{1,9},{5,13},{9,1},{13,5},{2,10},{6,14},... | collective-permute-start | bytes 1572872 | tf_op jit(solution)/shard_map/ppermute | solution.py:211
  15.6 71.4 %collective-permute-start.2 = (bf16[4,128,512]{2,1,0:T(8,128)(2,1)S(1)}, bf16[4,128,512]{2,1,0:T(8,128)(2,1)S(1)}, u32[]{:S(2)}, u32[]{:S(2)}) collective-permute-start(bf16[4,128,512]{2,1,0:T(8,128)(2,1)S(1)} %bitcast.47), channel_id=1, source_target_pairs={{0,12},{4,0},{8,4},{12,8},{1,13},{5,1},{9,5},{13,9},{2,14},{6,2},{... | collective-permute-start | bytes 1572872 | tf_op jit(solution)/shard_map/ppermute | solution.py:211
  86.7 14.4 %collective-permute-start.12 = (bf16[128,2048]{1,0:T(8,128)(2,1)S(1)}, bf16[128,2048]{1,0:T(8,128)(2,1)S(1)}, u32[]{:S(2)}, u32[]{:S(2)}) collective-permute-start(bf16[128,2048]{1,0:T(8,128)(2,1)S(1)} %bitcast.43), channel_id=1, source_target_pairs={{0,12},{4,0},{8,4},{12,8},{1,13},{5,1},{9,5},{13,9},{2,14},{6,2},{... | collective-permute-start | bytes 1572872 | tf_op jit(solution)/shard_map/ppermute | solution.py:211
  87.1 14.1 %collective-permute-start.44 = (bf16[128,2048]{1,0:T(8,128)(2,1)S(1)}, bf16[128,2048]{1,0:T(8,128)(2,1)S(1)}, u32[]{:S(2)}, u32[]{:S(2)}) collective-permute-start(bf16[128,2048]{1,0:T(8,128)(2,1)S(1)} %bitcast.44), channel_id=1, source_target_pairs={{0,2},{1,3},{2,0},{3,1},{4,6},{5,7},{6,4},{7,5},{8,10},{9,11},{10,... | collective-permute-start | bytes 1572872 | tf_op jit(solution)/shard_map/ppermute | solution.py:215
  94.0 13.5 %collective-permute-start.26 = (bf16[128,2048]{1,0:T(8,128)(2,1)S(1)}, bf16[128,2048]{1,0:T(8,128)(2,1)S(1)}, u32[]{:S(2)}, u32[]{:S(2)}) collective-permute-start(bf16[128,2048]{1,0:T(8,128)(2,1)S(1)} %bitcast.46), channel_id=1, source_target_pairs={{0,16},{16,0},{1,17},{17,1},{2,18},{18,2},{3,19},{19,3},{4,20},{20... | collective-permute-start | bytes 1572872 | tf_op jit(solution)/shard_map/ppermute | solution.py:215
  94.3 19.4 %collective-permute-start.3 = (bf16[512,512]{1,0:T(8,128)(2,1)}, bf16[512,512]{1,0:T(8,128)(2,1)S(1)}, u32[]{:S(2)}, u32[]{:S(2)}) collective-permute-start(bf16[512,512]{1,0:T(8,128)(2,1)} %attend.1.refs_5_), channel_id=1, source_target_pairs={{0,4},{4,8},{8,12},{12,0},{1,5},{5,9},{9,13},{13,1},{2,6},{6,10},{... | collective-permute-start | bytes 1572872 | tf_op jit(solution)/shard_map/ppermute | solution.py:211
  101.1 46.3 %collective-permute-start.4 = (bf16[512,512]{1,0:T(8,128)(2,1)}, bf16[512,512]{1,0:T(8,128)(2,1)S(1)}, u32[]{:S(2)}, u32[]{:S(2)}) collective-permute-start(bf16[512,512]{1,0:T(8,128)(2,1)} %attend.1.refs_5_), channel_id=1, source_target_pairs={{0,8},{4,12},{8,0},{12,4},{1,9},{5,13},{9,1},{13,5},{2,10},{6,14},... | collective-permute-start | bytes 1572872 | tf_op jit(solution)/shard_map/ppermute | solution.py:211
  101.1 46.8 %collective-permute-start.5 = (bf16[512,512]{1,0:T(8,128)(2,1)}, bf16[512,512]{1,0:T(8,128)(2,1)S(1)}, u32[]{:S(2)}, u32[]{:S(2)}) collective-permute-start(bf16[512,512]{1,0:T(8,128)(2,1)} %attend.1.refs_5_), channel_id=1, source_target_pairs={{0,12},{4,0},{8,4},{12,8},{1,13},{5,1},{9,5},{13,9},{2,14},{6,2},{... | collective-permute-start | bytes 1572872 | tf_op jit(solution)/shard_map/ppermute | solution.py:211
  101.5 47.3 %collective-permute-start.34 = (bf16[512,512]{1,0:T(8,128)(2,1)}, bf16[512,512]{1,0:T(8,128)(2,1)S(1)}, u32[]{:S(2)}, u32[]{:S(2)}) collective-permute-start(bf16[512,512]{1,0:T(8,128)(2,1)} %attend.1.refs_5_), channel_id=1, source_target_pairs={{0,2},{1,3},{2,0},{3,1},{4,6},{5,7},{6,4},{7,5},{8,10},{9,11},{10,... | collective-permute-start | bytes 1572872 | tf_op jit(solution)/shard_map/ppermute | solution.py:215
  107.5 41.3 %collective-permute-start.47 = (bf16[128,2048]{1,0:T(8,128)(2,1)S(1)}, bf16[128,2048]{1,0:T(8,128)(2,1)S(1)}, u32[]{:S(2)}, u32[]{:S(2)}) collective-permute-start(bf16[128,2048]{1,0:T(8,128)(2,1)S(1)} %collective-permute-done.11.refs_15_), channel_id=1, source_target_pairs={{0,2},{1,3},{2,0},{3,1},{4,6},{5,7},{6,4},{7,5},{8,10},{9,11},{10,... | collective-permute-start | bytes 1572872 | tf_op jit(solution)/shard_map/ppermute | solution.py:215
  113.7 35.6 %collective-permute-start.60 = (bf16[128,2048]{1,0:T(8,128)(2,1)S(1)}, bf16[128,2048]{1,0:T(8,128)(2,1)S(1)}, u32[]{:S(2)}, u32[]{:S(2)}) collective-permute-start(bf16[128,2048]{1,0:T(8,128)(2,1)S(1)} %collective-permute-done.10.refs_14_), channel_id=1, source_target_pairs={{0,2},{1,3},{2,0},{3,1},{4,6},{5,7},{6,4},{7,5},{8,10},{9,11},{10,... | collective-permute-start | bytes 1572872 | tf_op jit(solution)/shard_map/ppermute | solution.py:215
  147.4 13.0 %collective-permute-start.61 = (bf16[128,2048]{1,0:T(8,128)(2,1)S(1)}, bf16[128,2048]{1,0:T(8,128)(2,1)S(1)}, u32[]{:S(2)}, u32[]{:S(2)}) collective-permute-start(bf16[128,2048]{1,0:T(8,128)(2,1)S(1)} %collective-permute-done.12.refs_16_), channel_id=1, source_target_pairs={{0,2},{1,3},{2,0},{3,1},{4,6},{5,7},{6,4},{7,5},{8,10},{9,11},{10,... | collective-permute-start | bytes 1572872 | tf_op jit(solution)/shard_map/ppermute | solution.py:215
  148.0 13.8 %collective-permute-start.62 = (bf16[128,2048]{1,0:T(8,128)(2,1)S(1)}, bf16[128,2048]{1,0:T(8,128)(2,1)S(1)}, u32[]{:S(2)}, u32[]{:S(2)}) collective-permute-start(bf16[128,2048]{1,0:T(8,128)(2,1)S(1)} %collective-permute-done.44.refs_13_), channel_id=1, source_target_pairs={{0,1},{1,0},{2,3},{3,2},{4,5},{5,4},{6,7},{7,6},{8,9},{9,8},{10,11... | collective-permute-start | bytes 1572872 | tf_op jit(solution)/shard_map/ppermute | solution.py:215
  148.7 13.3 %collective-permute-start.6 = (bf16[512,512]{1,0:T(8,128)(2,1)}, bf16[512,512]{1,0:T(8,128)(2,1)}, u32[]{:S(2)}, u32[]{:S(2)}) collective-permute-start(bf16[512,512]{1,0:T(8,128)(2,1)} %attend.1.refs_5_), channel_id=1, source_target_pairs={{0,1},{1,0},{2,3},{3,2},{4,5},{5,4},{6,7},{7,6},{8,9},{9,8},{10,11... | collective-permute-start | bytes 1572872 | tf_op jit(solution)/shard_map/ppermute | solution.py:215
  148.8 14.4 %collective-permute-start.14 = (bf16[128,2048]{1,0:T(8,128)(2,1)S(1)}, bf16[128,2048]{1,0:T(8,128)(2,1)S(1)}, u32[]{:S(2)}, u32[]{:S(2)}) collective-permute-start(bf16[128,2048]{1,0:T(8,128)(2,1)S(1)} %collective-permute-done.10.refs_14_), channel_id=1, source_target_pairs={{0,1},{1,0},{2,3},{3,2},{4,5},{5,4},{6,7},{7,6},{8,9},{9,8},{10,11... | collective-permute-start | bytes 1572872 | tf_op jit(solution)/shard_map/ppermute | solution.py:215
  149.3 14.8 %collective-permute-start.15 = (bf16[128,2048]{1,0:T(8,128)(2,1)S(1)}, bf16[128,2048]{1,0:T(8,128)(2,1)S(1)}, u32[]{:S(2)}, u32[]{:S(2)}) collective-permute-start(bf16[128,2048]{1,0:T(8,128)(2,1)S(1)} %collective-permute-done.11.refs_15_), channel_id=1, source_target_pairs={{0,1},{1,0},{2,3},{3,2},{4,5},{5,4},{6,7},{7,6},{8,9},{9,8},{10,11... | collective-permute-start | bytes 1572872 | tf_op jit(solution)/shard_map/ppermute | solution.py:215
  161.7 13.5 %collective-permute-start.27 = (bf16[128,2048]{1,0:T(8,128)(2,1)S(1)}, bf16[128,2048]{1,0:T(8,128)(2,1)S(1)}, u32[]{:S(2)}, u32[]{:S(2)}) collective-permute-start(bf16[128,2048]{1,0:T(8,128)(2,1)S(1)} %collective-permute-done.10.refs_14_), channel_id=1, source_target_pairs={{0,16},{16,0},{1,17},{17,1},{2,18},{18,2},{3,19},{19,3},{4,20},{20... | collective-permute-start | bytes 1572872 | tf_op jit(solution)/shard_map/ppermute | solution.py:215
  162.0 24.5 %collective-permute-start.29 = (bf16[128,2048]{1,0:T(8,128)(2,1)S(1)}, bf16[128,2048]{1,0:T(8,128)(2,1)S(1)}, u32[]{:S(2)}, u32[]{:S(2)}) collective-permute-start(bf16[128,2048]{1,0:T(8,128)(2,1)S(1)} %collective-permute-done.12.refs_16_), channel_id=1, source_target_pairs={{0,16},{16,0},{1,17},{17,1},{2,18},{18,2},{3,19},{19,3},{4,20},{20... | collective-permute-start | bytes 1572872 | tf_op jit(solution)/shard_map/ppermute | solution.py:215
  163.2 34.5 %collective-permute-start.45 = (bf16[128,2048]{1,0:T(8,128)(2,1)S(1)}, bf16[128,2048]{1,0:T(8,128)(2,1)S(1)}, u32[]{:S(2)}, u32[]{:S(2)}) collective-permute-start(bf16[128,2048]{1,0:T(8,128)(2,1)S(1)} %collective-permute-done.44.refs_13_), channel_id=1, source_target_pairs={{0,16},{16,0},{1,17},{17,1},{2,18},{18,2},{3,19},{19,3},{4,20},{20... | collective-permute-start | bytes 1572872 | tf_op jit(solution)/shard_map/ppermute | solution.py:215
  164.1 44.9 %collective-permute-start.18 = (bf16[512,512]{1,0:T(8,128)(2,1)}, bf16[512,512]{1,0:T(8,128)(2,1)S(1)}, u32[]{:S(2)}, u32[]{:S(2)}) collective-permute-start(bf16[512,512]{1,0:T(8,128)(2,1)} %attend.1.refs_5_), channel_id=1, source_target_pairs={{0,16},{16,0},{1,17},{17,1},{2,18},{18,2},{3,19},{19,3},{4,20},{20... | collective-permute-start | bytes 1572872 | tf_op jit(solution)/shard_map/ppermute | solution.py:215
  164.9 55.3 %collective-permute-start.28 = (bf16[128,2048]{1,0:T(8,128)(2,1)S(1)}, bf16[128,2048]{1,0:T(8,128)(2,1)S(1)}, u32[]{:S(2)}, u32[]{:S(2)}) collective-permute-start(bf16[128,2048]{1,0:T(8,128)(2,1)S(1)} %collective-permute-done.11.refs_15_), channel_id=1, source_target_pairs={{0,16},{16,0},{1,17},{17,1},{2,18},{18,2},{3,19},{19,3},{4,20},{20... | collective-permute-start | bytes 1572872 | tf_op jit(solution)/shard_map/ppermute | solution.py:215
  175.3 45.8 %collective-permute-start.30 = (bf16[128,2048]{1,0:T(8,128)(2,1)S(1)}, bf16[128,2048]{1,0:T(8,128)(2,1)S(1)}, u32[]{:S(2)}, u32[]{:S(2)}) collective-permute-start(bf16[128,2048]{1,0:T(8,128)(2,1)S(1)} %collective-permute-done.26.refs_13_), channel_id=1, source_target_pairs={{0,1},{1,0},{2,3},{3,2},{4,5},{5,4},{6,7},{7,6},{8,9},{9,8},{10,11... | collective-permute-start | bytes 1572872 | tf_op jit(solution)/shard_map/ppermute | solution.py:215
  186.5 34.7 %collective-permute-start.54 = (bf16[512,512]{1,0:T(8,128)(2,1)S(1)}, bf16[512,512]{1,0:T(8,128)(2,1)S(1)}, u32[]{:S(2)}, u32[]{:S(2)}) collective-permute-start(bf16[512,512]{1,0:T(8,128)(2,1)S(1)} %collective-permute-done.3.refs_6_), channel_id=1, source_target_pairs={{0,2},{1,3},{2,0},{3,1},{4,6},{5,7},{6,4},{7,5},{8,10},{9,11},{10,... | collective-permute-start | bytes 1572872 | tf_op jit(solution)/shard_map/ppermute | solution.py:215
  197.7 23.9 %collective-permute-start.37 = (bf16[512,512]{1,0:T(8,128)(2,1)S(1)}, bf16[512,512]{1,0:T(8,128)(2,1)S(1)}, u32[]{:S(2)}, u32[]{:S(2)}) collective-permute-start(bf16[512,512]{1,0:T(8,128)(2,1)S(1)} %collective-permute-done.4.refs_7_), channel_id=1, source_target_pairs={{0,2},{1,3},{2,0},{3,1},{4,6},{5,7},{6,4},{7,5},{8,10},{9,11},{10,... | collective-permute-start | bytes 1572872 | tf_op jit(solution)/shard_map/ppermute | solution.py:215
  209.0 12.8 %collective-permute-start.55 = (bf16[512,512]{1,0:T(8,128)(2,1)S(1)}, bf16[512,512]{1,0:T(8,128)(2,1)S(1)}, u32[]{:S(2)}, u32[]{:S(2)}) collective-permute-start(bf16[512,512]{1,0:T(8,128)(2,1)S(1)} %collective-permute-done.5.refs_8_), channel_id=1, source_target_pairs={{0,2},{1,3},{2,0},{3,1},{4,6},{5,7},{6,4},{7,5},{8,10},{9,11},{10,... | collective-permute-start | bytes 1572872 | tf_op jit(solution)/shard_map/ppermute | solution.py:215
  224.1 13.1 %collective-permute-start.19 = (bf16[512,512]{1,0:T(8,128)(2,1)S(1)}, bf16[512,512]{1,0:T(8,128)(2,1)S(1)}, u32[]{:S(2)}, u32[]{:S(2)}) collective-permute-start(bf16[512,512]{1,0:T(8,128)(2,1)S(1)} %collective-permute-done.3.refs_6_), channel_id=1, source_target_pairs={{0,16},{16,0},{1,17},{17,1},{2,18},{18,2},{3,19},{19,3},{4,20},{20... | collective-permute-start | bytes 1572872 | tf_op jit(solution)/shard_map/ppermute | solution.py:215
  224.8 23.7 %collective-permute-start.21 = (bf16[512,512]{1,0:T(8,128)(2,1)S(1)}, bf16[512,512]{1,0:T(8,128)(2,1)S(1)}, u32[]{:S(2)}, u32[]{:S(2)}) collective-permute-start(bf16[512,512]{1,0:T(8,128)(2,1)S(1)} %collective-permute-done.5.refs_8_), channel_id=1, source_target_pairs={{0,16},{16,0},{1,17},{17,1},{2,18},{18,2},{3,19},{19,3},{4,20},{20... | collective-permute-start | bytes 1572872 | tf_op jit(solution)/shard_map/ppermute | solution.py:215
  225.6 34.1 %collective-permute-start.35 = (bf16[512,512]{1,0:T(8,128)(2,1)S(1)}, bf16[512,512]{1,0:T(8,128)(2,1)S(1)}, u32[]{:S(2)}, u32[]{:S(2)}) collective-permute-start(bf16[512,512]{1,0:T(8,128)(2,1)S(1)} %collective-permute-done.34.refs_5_), channel_id=1, source_target_pairs={{0,16},{16,0},{1,17},{17,1},{2,18},{18,2},{3,19},{19,3},{4,20},{20... | collective-permute-start | bytes 1572872 | tf_op jit(solution)/shard_map/ppermute | solution.py:215
  226.4 33.6 %collective-permute-start.46 = (bf16[128,2048]{1,0:T(8,128)(2,1)S(1)}, bf16[128,2048]{1,0:T(8,128)(2,1)S(1)}, u32[]{:S(2)}, u32[]{:S(2)}) collective-permute-start(bf16[128,2048]{1,0:T(8,128)(2,1)S(1)} %collective-permute-done.27.refs_14_), channel_id=1, source_target_pairs={{0,2},{1,3},{2,0},{3,1},{4,6},{5,7},{6,4},{7,5},{8,10},{9,11},{10,... | collective-permute-start | bytes 1572872 | tf_op jit(solution)/shard_map/ppermute | solution.py:215
  227.1 44.0 %collective-permute-start.48 = (bf16[128,2048]{1,0:T(8,128)(2,1)S(1)}, bf16[128,2048]{1,0:T(8,128)(2,1)}, u32[]{:S(2)}, u32[]{:S(2)}) collective-permute-start(bf16[128,2048]{1,0:T(8,128)(2,1)S(1)} %collective-permute-done.47.refs_15_), channel_id=1, source_target_pairs={{0,16},{16,0},{1,17},{17,1},{2,18},{18,2},{3,19},{19,3},{4,20},{20... | collective-permute-start | bytes 1572872 | tf_op jit(solution)/shard_map/ppermute | solution.py:215
  237.2 35.8 %collective-permute-start.49 = (bf16[128,2048]{1,0:T(8,128)(2,1)S(1)}, bf16[128,2048]{1,0:T(8,128)(2,1)}, u32[]{:S(2)}, u32[]{:S(2)}) collective-permute-start(bf16[128,2048]{1,0:T(8,128)(2,1)S(1)} %collective-permute-done.29.refs_16_), channel_id=1, source_target_pairs={{0,2},{1,3},{2,0},{3,1},{4,6},{5,7},{6,4},{7,5},{8,10},{9,11},{10,... | collective-permute-start | bytes 1572872 | tf_op jit(solution)/shard_map/ppermute | solution.py:215
  248.6 24.5 %collective-permute-start.50 = (bf16[128,2048]{1,0:T(8,128)(2,1)S(1)}, bf16[128,2048]{1,0:T(8,128)(2,1)S(1)}, u32[]{:S(2)}, u32[]{:S(2)}) collective-permute-start(bf16[128,2048]{1,0:T(8,128)(2,1)S(1)} %collective-permute-done.45.refs_13_), channel_id=1, source_target_pairs={{0,1},{1,0},{2,3},{3,2},{4,5},{5,4},{6,7},{7,6},{8,9},{9,8},{10,11... | collective-permute-start | bytes 1572872 | tf_op jit(solution)/shard_map/ppermute | solution.py:215
  259.7 22.5 %collective-permute-start.20 = (bf16[512,512]{1,0:T(8,128)(2,1)S(1)}, bf16[512,512]{1,0:T(8,128)(2,1)S(1)}, u32[]{:S(2)}, u32[]{:S(2)}) collective-permute-start(bf16[512,512]{1,0:T(8,128)(2,1)S(1)} %collective-permute-done.4.refs_7_), channel_id=1, source_target_pairs={{0,16},{16,0},{1,17},{17,1},{2,18},{18,2},{3,19},{19,3},{4,20},{20... | collective-permute-start | bytes 1572872 | tf_op jit(solution)/shard_map/ppermute | solution.py:215
  259.9 23.4 %collective-permute-start.22 = (bf16[512,512]{1,0:T(8,128)(2,1)S(1)}, bf16[512,512]{1,0:T(8,128)(2,1)S(1)}, u32[]{:S(2)}, u32[]{:S(2)}) collective-permute-start(bf16[512,512]{1,0:T(8,128)(2,1)S(1)} %collective-permute-done.18.refs_5_), channel_id=1, source_target_pairs={{0,1},{1,0},{2,3},{3,2},{4,5},{5,4},{6,7},{7,6},{8,9},{9,8},{10,11... | collective-permute-start | bytes 1572872 | tf_op jit(solution)/shard_map/ppermute | solution.py:215
  284.1 13.7 %collective-permute-start.36 = (bf16[512,512]{1,0:T(8,128)(2,1)S(1)}, bf16[512,512]{1,0:T(8,128)(2,1)}, u32[]{:S(2)}, u32[]{:S(2)}) collective-permute-start(bf16[512,512]{1,0:T(8,128)(2,1)S(1)} %collective-permute-done.19.refs_6_), channel_id=1, source_target_pairs={{0,2},{1,3},{2,0},{3,1},{4,6},{5,7},{6,4},{7,5},{8,10},{9,11},{10,... | collective-permute-start | bytes 1572872 | tf_op jit(solution)/shard_map/ppermute | solution.py:215
  284.7 14.3 %collective-permute-start.38 = (bf16[512,512]{1,0:T(8,128)(2,1)S(1)}, bf16[512,512]{1,0:T(8,128)(2,1)}, u32[]{:S(2)}, u32[]{:S(2)}) collective-permute-start(bf16[512,512]{1,0:T(8,128)(2,1)S(1)} %collective-permute-done.37.refs_7_), channel_id=1, source_target_pairs={{0,16},{16,0},{1,17},{17,1},{2,18},{18,2},{3,19},{19,3},{4,20},{20... | collective-permute-start | bytes 1572872 | tf_op jit(solution)/shard_map/ppermute | solution.py:215
  285.1 24.0 %collective-permute-start.39 = (bf16[512,512]{1,0:T(8,128)(2,1)S(1)}, bf16[512,512]{1,0:T(8,128)(2,1)}, u32[]{:S(2)}, u32[]{:S(2)}) collective-permute-start(bf16[512,512]{1,0:T(8,128)(2,1)S(1)} %collective-permute-done.21.refs_8_), channel_id=1, source_target_pairs={{0,2},{1,3},{2,0},{3,1},{4,6},{5,7},{6,4},{7,5},{8,10},{9,11},{10,... | collective-permute-start | bytes 1572872 | tf_op jit(solution)/shard_map/ppermute | solution.py:215
  286.0 23.8 %collective-permute-start.40 = (bf16[512,512]{1,0:T(8,128)(2,1)S(1)}, bf16[512,512]{1,0:T(8,128)(2,1)S(1)}, u32[]{:S(2)}, u32[]{:S(2)}) collective-permute-start(bf16[512,512]{1,0:T(8,128)(2,1)S(1)} %collective-permute-done.35.refs_5_), channel_id=1, source_target_pairs={{0,1},{1,0},{2,3},{3,2},{4,5},{5,4},{6,7},{7,6},{8,9},{9,8},{10,11... | collective-permute-start | bytes 1572872 | tf_op jit(solution)/shard_map/ppermute | solution.py:215
  287.0 23.0 %collective-permute-start.51 = (bf16[128,2048]{1,0:T(8,128)(2,1)S(1)}, bf16[128,2048]{1,0:T(8,128)(2,1)S(1)}, u32[]{:S(2)}, u32[]{:S(2)}) collective-permute-start(bf16[128,2048]{1,0:T(8,128)(2,1)S(1)} %collective-permute-done.46.refs_14_), channel_id=1, source_target_pairs={{0,1},{1,0},{2,3},{3,2},{4,5},{5,4},{6,7},{7,6},{8,9},{9,8},{10,11... | collective-permute-start | bytes 1572872 | tf_op jit(solution)/shard_map/ppermute | solution.py:215
  297.8 12.7 %collective-permute-start.23 = (bf16[512,512]{1,0:T(8,128)(2,1)S(1)}, bf16[512,512]{1,0:T(8,128)(2,1)S(1)}, u32[]{:S(2)}, u32[]{:S(2)}) collective-permute-start(bf16[512,512]{1,0:T(8,128)(2,1)S(1)} %collective-permute-done.19.refs_6_), channel_id=1, source_target_pairs={{0,1},{1,0},{2,3},{3,2},{4,5},{5,4},{6,7},{7,6},{8,9},{9,8},{10,11... | collective-permute-start | bytes 1572872 | tf_op jit(solution)/shard_map/ppermute | solution.py:215
  309.8 67.0 %collective-permute-start.52 = (bf16[128,2048]{1,0:T(8,128)(2,1)}, bf16[128,2048]{1,0:T(8,128)(2,1)}, u32[]{:S(2)}, u32[]{:S(2)}) collective-permute-start(bf16[128,2048]{1,0:T(8,128)(2,1)} %collective-permute-done.48.refs_15_), channel_id=1, source_target_pairs={{0,1},{1,0},{2,3},{3,2},{4,5},{5,4},{6,7},{7,6},{8,9},{9,8},{10,11... | collective-permute-start | bytes 1572872 | tf_op jit(solution)/shard_map/ppermute | solution.py:215
  309.9 66.9 %collective-permute-start.53 = (bf16[128,2048]{1,0:T(8,128)(2,1)}, bf16[128,2048]{1,0:T(8,128)(2,1)}, u32[]{:S(2)}, u32[]{:S(2)}) collective-permute-start(bf16[128,2048]{1,0:T(8,128)(2,1)} %collective-permute-done.49.refs_16_), channel_id=1, source_target_pairs={{0,1},{1,0},{2,3},{3,2},{4,5},{5,4},{6,7},{7,6},{8,9},{9,8},{10,11... | collective-permute-start | bytes 1572872 | tf_op jit(solution)/shard_map/ppermute | solution.py:215
  310.5 66.3 %collective-permute-start.41 = (bf16[512,512]{1,0:T(8,128)(2,1)}, bf16[512,512]{1,0:T(8,128)(2,1)}, u32[]{:S(2)}, u32[]{:S(2)}) collective-permute-start(bf16[512,512]{1,0:T(8,128)(2,1)} %collective-permute-done.36.refs_6_), channel_id=1, source_target_pairs={{0,1},{1,0},{2,3},{3,2},{4,5},{5,4},{6,7},{7,6},{8,9},{9,8},{10,11... | collective-permute-start | bytes 1572872 | tf_op jit(solution)/shard_map/ppermute | solution.py:215
  310.6 66.2 %collective-permute-start.42 = (bf16[512,512]{1,0:T(8,128)(2,1)}, bf16[512,512]{1,0:T(8,128)(2,1)}, u32[]{:S(2)}, u32[]{:S(2)}) collective-permute-start(bf16[512,512]{1,0:T(8,128)(2,1)} %collective-permute-done.38.refs_7_), channel_id=1, source_target_pairs={{0,1},{1,0},{2,3},{3,2},{4,5},{5,4},{6,7},{7,6},{8,9},{9,8},{10,11... | collective-permute-start | bytes 1572872 | tf_op jit(solution)/shard_map/ppermute | solution.py:215
  312.3 64.6 %collective-permute-start.43 = (bf16[512,512]{1,0:T(8,128)(2,1)}, bf16[512,512]{1,0:T(8,128)(2,1)}, u32[]{:S(2)}, u32[]{:S(2)}) collective-permute-start(bf16[512,512]{1,0:T(8,128)(2,1)} %collective-permute-done.39.refs_8_), channel_id=1, source_target_pairs={{0,1},{1,0},{2,3},{3,2},{4,5},{5,4},{6,7},{7,6},{8,9},{9,8},{10,11... | collective-permute-start | bytes 1572872 | tf_op jit(solution)/shard_map/ppermute | solution.py:215
  (77 other events, 3860.8 us)

commit v2 on v1

v2 whole, which is shorter than its diff:
```python
import math

import jax
import jax.numpy as jnp
from jax import lax
from jax.experimental import pallas as pl
from jax.experimental.pallas import tpu as pltpu
from jax.sharding import PartitionSpec as P

HEAD_DIM = 128
F32 = jnp.float32
BF16 = jnp.bfloat16
VMEM_LIMIT = 56 * 1024 * 1024


VMEM_SPEC = pl.BlockSpec(memory_space=pltpu.VMEM)
SMEM_SPEC = pl.BlockSpec(memory_space=pltpu.SMEM)
NN = (((1,), (0,)), ((), ()))


def on_chip(body, shapes, name, args, scratch=(), scalars=0):
    return pl.pallas_call(
        body,
        out_shape=shapes,
        in_specs=[SMEM_SPEC] * scalars + [VMEM_SPEC] * (len(args) - scalars),
        out_specs=jax.tree.map(lambda _: VMEM_SPEC, shapes),
        scratch_shapes=list(scratch),
        compiler_params=pltpu.CompilerParams(vmem_limit_bytes=VMEM_LIMIT),
        name=name,
    )(*args)


def pack_heads(arrays, ctx):
    tokens, width_all = arrays[0].shape
    width = width_all // ctx

    def body(*refs):
        for i, ref in enumerate(refs[:-1]):
            for j in range(ctx):
                refs[-1][j, i] = ref[:, j * width : (j + 1) * width]

    shape = jax.ShapeDtypeStruct((ctx, len(arrays), tokens, width), BF16)
    return on_chip(body, shape, "pack_heads", arrays)


def attend(packs):
    ctx, _, tokens, width = packs.shape
    scale = 1.0 / math.sqrt(HEAD_DIM)
    nt = (((1,), (1,)), ((), ()))

    def body(packs, out):
        for h in range(width // HEAD_DIM):
            cols = slice(h * HEAD_DIM, (h + 1) * HEAD_DIM)
            q, k, v = (
                jnp.concatenate([packs[j, i, :, cols] for j in range(ctx)], axis=0)
                for i in range(3)
            )
            scores = lax.dot_general(q, k, nt, preferred_element_type=F32) * scale
            largest = jnp.max(scores, axis=1, keepdims=True)
            powers = jnp.exp(scores - largest)
            probs = (powers / jnp.sum(powers, axis=1, keepdims=True)).astype(BF16)
            attended = lax.dot_general(probs, v, NN, preferred_element_type=F32)
            for j in range(ctx):
                rows = slice(j * tokens, (j + 1) * tokens)
                out[rows, cols] = (packs[j, 3, :, cols].astype(F32) + attended[rows]).astype(BF16)

    return on_chip(body, jax.ShapeDtypeStruct((ctx * tokens, width), BF16), "attend", [packs])


def selection(gate, cap):
    tokens = gate.shape[1]
    lower = lax.broadcasted_iota(jnp.int32, (tokens, tokens), 0)
    upper = lax.broadcasted_iota(jnp.int32, (tokens, tokens), 1)
    running = (lower <= upper).astype(BF16)
    row_number = lax.broadcasted_iota(jnp.int32, (cap, tokens), 0).astype(F32)
    picked = gate != 0.0
    marks = jnp.broadcast_to(picked.astype(F32), (8, tokens)).astype(BF16)
    rank = lax.dot_general(marks, running, NN, preferred_element_type=F32)[:1]
    return jnp.logical_and(row_number + 1.0 == rank, picked)


def cot_rows(place, down, blocks, cap, parts):
    seqs, (ctx, rows_in, width_all) = len(blocks), blocks[0].shape
    tokens = rows_in - 8
    half, hidden_width = width_all // parts, down.shape[1]
    count = seqs * ctx * cap

    def body(place, down, *refs):
        inputs, (cot_out, back_out, column_out, gate_out, cot_ref) = refs[:seqs], refs[seqs:]
        column = pl.ds(pl.multiple_of(place[2] * tokens, tokens), tokens)
        for i in range(seqs):
            for t in range(ctx):
                terms = inputs[i][t, tokens : tokens + 8, column].astype(F32)
                gate = terms[0:1] + terms[1:2] + terms[2:3]
                gate_out[i * ctx + t] = gate
                chosen = selection(gate, cap)
                select = chosen.astype(F32).astype(BF16)
                at = (i * ctx + t) * cap
                column_out[at : at + cap, :] = jnp.broadcast_to(
                    jnp.sum(jnp.where(chosen, gate, 0.0), axis=1, keepdims=True), (cap, 128)
                )
                for p in range(parts):
                    block = inputs[i][t, :tokens, p * half : (p + 1) * half]
                    rows = lax.dot_general(select, block, NN, preferred_element_type=F32)
                    cot_ref[p, at : at + cap, :] = rows.astype(BF16)
        back = None
        for p in range(parts):
            term = lax.dot_general(
                cot_ref[p], down[p * half : (p + 1) * half, :], NN, preferred_element_type=F32
            )
            back = term if back is None else back + term
        back_out[...] = back * column_out[:, :1]
        cot_out[...] = cot_ref[place[1]]

    shapes = [
        jax.ShapeDtypeStruct((count, half), BF16),
        jax.ShapeDtypeStruct((count, hidden_width), F32),
        jax.ShapeDtypeStruct((count, 128), F32),
        jax.ShapeDtypeStruct((seqs * ctx, 1, tokens), F32),
    ]
    scratch = [pltpu.VMEM((parts, count, half), BF16)]
    return on_chip(body, shapes, "cot_rows", [place, down, *blocks], scratch, 1)


def stream_rows(place, gain, gate_up, slices, back, columns, gates, cap, parts):
    seqs, (ctx, length, width) = len(slices), slices[0].shape
    tokens, width_all = length // ctx, width * ctx
    half, hidden_width = width_all // parts, back.shape[1]
    count = seqs * ctx * cap

    def body(place, gain, gate_up, back_in, columns, gates, *refs):
        inputs, (norm_out, back_out, hidden_out, rows_ref) = refs[:seqs], refs[seqs:]
        for i in range(seqs):
            for t in range(ctx):
                first = pl.multiple_of(place[3 + t] * tokens, tokens)
                select = selection(gates[i * ctx + t], cap).astype(F32).astype(BF16)
                at = (i * ctx + t) * cap
                for f in range(ctx):
                    block = inputs[i][f, pl.ds(first, tokens), :]
                    rows = lax.dot_general(select, block, NN, preferred_element_type=F32)
                    rows_ref[place[3 + f], at : at + cap, :] = rows.astype(BF16)
        total = None
        for f in range(ctx):
            wide = rows_ref[f].astype(F32)
            square = jnp.sum(wide * wide, axis=1, keepdims=True)
            total = square if total is None else total + square
        factor = lax.rsqrt(total / width_all + 1e-05)
        proj = None
        for f in range(ctx):
            normed = (rows_ref[f].astype(F32) * factor * gain[f]).astype(BF16)
            rows_ref[f] = normed
            term = lax.dot_general(
                normed, gate_up[f * width : (f + 1) * width, :], NN, preferred_element_type=F32
            )
            proj = term if proj is None else proj + term
        gate_part, up_part = proj[:, :hidden_width], proj[:, hidden_width:]
        sigma = 1.0 / (1.0 + jnp.exp(-gate_part))
        activated = gate_part * sigma
        back = back_in[...]
        hidden_out[...] = (activated * up_part * columns[:, :1]).astype(BF16)
        slope = sigma * (1.0 + gate_part * (1.0 - sigma))
        back_out[:, :hidden_width] = (back * up_part * slope).astype(BF16)
        back_out[:, hidden_width:] = (back * activated).astype(BF16)
        each = ctx // parts
        for f in range(each):
            norm_out[:, f * width : (f + 1) * width] = rows_ref[place[1] * each + f]

    shapes = [
        jax.ShapeDtypeStruct((count, half), BF16),
        jax.ShapeDtypeStruct((count, 2 * hidden_width), BF16),
        jax.ShapeDtypeStruct((count, hidden_width), BF16),
    ]
    scratch = [pltpu.VMEM((ctx, count, width), BF16)]
    args = [place, gain, gate_up, back, columns, gates, *slices]
    return on_chip(body, shapes, "stream_rows", args, scratch, 1)


def own_rows(place, slices):
    ctx, length, width = slices.shape
    tokens = length // ctx

    def body(place, slices, out, rows_ref):
        own = pl.ds(pl.multiple_of(place[0] * tokens, tokens), tokens)
        for f in range(ctx):
            rows_ref[place[3 + f]] = slices[f, own, :]
        for f in range(ctx):
            out[:, f * width : (f + 1) * width] = rows_ref[f]

    shape = jax.ShapeDtypeStruct((tokens, ctx * width), BF16)
    scratch = [pltpu.VMEM((ctx, tokens, width), BF16)]
    return on_chip(body, shape, "own_rows", [place, slices], scratch, 1)


def grads_kernel(*refs, groups, add):
    norms, cots, backs, hiddens = (refs[i * groups : (i + 1) * groups] for i in range(4))
    rest = refs[4 * groups :]
    tn = (((0,), (0,)), ((), ()))

    def whole(parts):
        return jnp.concatenate([p[...] for p in parts], axis=0)

    left = lax.dot_general(whole(norms), whole(backs), tn, preferred_element_type=F32)
    right = lax.dot_general(whole(cots), whole(hiddens), tn, preferred_element_type=F32)
    out_left, out_right = rest[-2:]
    if add:
        left = left + rest[0][0]
        right = right + rest[1][0]
    out_left[0] = left
    out_right[0] = right


def grads(pieces, before):
    groups = len(pieces)
    norms, cots, backs, hiddens = zip(*pieces)
    count, half = norms[0].shape
    step = 256
    tall = [pl.BlockSpec((count, step), lambda i: (0, i))] * groups
    out_widths = (backs[0].shape[1], hiddens[0].shape[1])
    full = [
        pl.BlockSpec((count, w), lambda i: (0, 0)) for w in out_widths for _ in range(groups)
    ]
    outs = [pl.BlockSpec((1, step, w), lambda i: (0, i, 0)) for w in out_widths]
    add = before is not None
    args = [*norms, *cots, *backs, *hiddens] + (list(before) if add else [])
    return pl.pallas_call(
        lambda *refs: grads_kernel(*refs, groups=groups, add=add),
        out_shape=[jax.ShapeDtypeStruct((1, half, w), F32) for w in out_widths],
        grid=(half // step,),
        in_specs=tall + tall + full + (outs if add else []),
        out_specs=outs,
        input_output_aliases={4 * groups: 0, 4 * groups + 1: 1} if add else {},
        compiler_params=pltpu.CompilerParams(vmem_limit_bytes=VMEM_LIMIT),
        name="grads",
    )(*args)


def shifted(value, axis, step, count):
    return lax.ppermute(value, axis, [(i, (i + step) % count) for i in range(count)])


def flipped(value, axis, mask, count):
    return lax.ppermute(value, axis, [(i, i ^ mask) for i in range(count)])


def after(value, *others):
    return lax.optimization_barrier((value, *others))[0]


SOURCES = ((0, 1, 2, 3), (1, 0, 1, 2), (2, 2, 3, 1), (3, 3, 0, 0))


def spread(own, z, exp, cut, waits=None, midway=None):
    waits = waits or {}

    def ready(number, values):
        held = lax.optimization_barrier((values, waits.get(number, ())))
        return held[0]

    def up(value, pairs):
        return lax.ppermute(value, "ctx", pairs)

    def x(value):
        return flipped(value, "exp", 2, exp)

    def y(value):
        return flipped(value, "dp", 1, 2)

    def core(value):
        return flipped(value, "exp", 1, exp)

    count = own.shape[0]
    up1, down1 = up(own, [(0, 1), (1, 2), (2, 3)]), up(own, [(1, 0), (2, 1), (3, 2)])
    x0, y0 = x(own), y(own)
    up1, down1, x0, y0 = ready(2, (up1, down1, x0, y0))
    one = jnp.where(z == 0, down1, up1)
    up2, down2 = up(up1, [(1, 2), (2, 3)]), up(down1, [(1, 0), (2, 1)])
    x1 = x(jnp.concatenate([one, y0[cut:]]))
    y1 = y(jnp.concatenate([one, x0[:cut]]))
    up2, down2, x1, y1 = ready(3, (up2, down2, x1, y1))
    two = jnp.where(z == 3, up2, jnp.where(z == 0, down2, down1))
    middle = jnp.where(z == 2, up2, down2)
    ends = up(middle, [(1, 0), (2, 3)])
    x2 = x(jnp.concatenate([two, y1[cut:count]]))
    y2 = y(jnp.concatenate([two, x1[:cut]]))
    ends, x2, y2 = ready(4, (ends, x2, y2))
    three = jnp.where(jnp.logical_or(z == 0, z == 3), ends, middle)
    x3 = x(jnp.concatenate([three, y2[cut:count]]))
    y3 = y(jnp.concatenate([three, x2[:cut]]))
    mine = jnp.stack([own, one, two, three])
    mine_core = core(mine)
    x3, y3 = ready(5, (x3, y3))
    done = midway(mine, mine_core) if midway else ()
    x4, y4 = x(y3[cut:count]), y(x3[:cut])
    over_x = jnp.stack([x0, x1[:count], x2[:count], x3[:count]])
    over_y = jnp.stack([y0, y1[:count], y2[:count], y3[:count]])
    over_x_core, over_y_core = core(over_x), core(over_y)
    both = jnp.stack(
        [
            jnp.concatenate([a[-cut:], b[cut - count :]])
            for a, b in ((y1, x1), (y2, x2), (y3, x3), (y4, x4))
        ]
    )
    both = lax.optimization_barrier((both, done))[0]
    both_core = core(both)
    return {
        (0, 0): (mine, mine_core),
        (0, 1): (over_x, over_x_core),
        (1, 0): (over_y, over_y_core),
        (1, 1): (both, both_core),
    }


def gate_terms(value):
    terms = []
    for _ in range(3):
        term = lax.reduce_precision(value, 8, 7)
        terms.append(term.astype(BF16))
        value = value - term
    return terms


def expert_gates(routes, gates, flags, experts):
    named = routes[:, :, None] == jnp.arange(experts, dtype=jnp.int32)[None, None, :]
    scaled = gates * flags.astype(F32)[:, None]
    return jnp.sum(jnp.where(named, scaled[:, :, None], 0.0), axis=1)


def per_device(
    queries, keys, values, resid, norm_gain, expert_ids, gate_weights, mask_flags, cotangent, w_gate_up, w_down
):
    ctx, exp, parts = (lax.axis_size(a) for a in ("ctx", "exp", "dp"))
    z, e, part = (lax.axis_index(a) for a in ("ctx", "exp", "dp"))
    experts = ctx * exp
    _, tokens, width_all = queries.shape
    width = width_all // ctx
    most = min(tokens, tokens * expert_ids.shape[2] * 17 // (16 * experts))
    cap = -(-most // 16) * 16

    packed = pack_heads([queries[0], keys[0], values[0], resid[0]], ctx)
    packs = lax.all_to_all(packed, "ctx", split_axis=0, concat_axis=0, tiled=True)
    own_slice = attend(packs)

    by_expert = expert_gates(expert_ids[0], gate_weights[0], mask_flags[0], experts)
    terms = jnp.stack([t.T.reshape(experts * tokens) for t in gate_terms(by_expert)])
    terms = jnp.pad(terms, ((0, 5), (0, width_all - experts * tokens)))
    block = jnp.concatenate([cotangent[0], terms], axis=0)
    cots = spread(after(block, packed), z, exp, tokens // 2, {5: own_slice})

    sources = [jnp.asarray(row, jnp.int32)[z] for row in SOURCES]
    place = jnp.stack([z, part, z * exp + e, *sources]).astype(jnp.int32)
    gain = norm_gain.reshape(ctx, 1, width)
    order = ((0, 0), (0, 1), (1, 0), (1, 1))
    picked = {where: cot_rows(place, w_down[0], cots[where], cap, parts) for where in order}

    def expert(where, slices):
        rows, back, columns, gates = picked[where]
        normed, both, hidden = stream_rows(
            place, gain, w_gate_up[0], slices, back, columns, gates, cap, parts
        )
        return normed, rows, both, hidden

    pieces = {}

    def midway(mine, mine_core):
        pieces[0, 0] = expert((0, 0), (mine, mine_core))
        return pieces[0, 0]

    waits = {3: picked[0, 0], 4: picked[0, 1], 5: (picked[1, 0], picked[1, 1])}
    streams = spread(own_slice, z, exp, tokens * ctx // 2, waits, midway)
    for where in order[1:]:
        pieces[where] = expert(where, streams[where])
    stream = own_rows(place, streams[0, 0][0])
    first = grads([pieces[0, 0], pieces[0, 1]], None)
    left, right = grads([pieces[1, 0], pieces[1, 1]], first)
    return stream[None], left, right


def routed_device(
    queries, keys, values, resid, norm_gain, expert_ids, gate_weights, mask_flags, cotangent, w_gate_up, w_down
):
    ctx, exp = (lax.axis_size(a) for a in ("ctx", "exp"))
    experts = ctx * exp
    _, tokens, width_all = queries.shape
    top = expert_ids.shape[2]
    capacity = min(tokens, tokens * top * 17 // (16 * experts))
    keys_all = lax.all_gather(keys[0], "ctx", axis=0, tiled=True)
    values_all = lax.all_gather(values[0], "ctx", axis=0, tiled=True)
    heads = width_all // HEAD_DIM
    q, k, v = (a.reshape(-1, heads, HEAD_DIM) for a in (queries[0], keys_all, values_all))
    scores = jnp.einsum("qhd,khd->hqk", q, k, preferred_element_type=F32) / math.sqrt(HEAD_DIM)
    powers = jnp.exp(scores - jnp.max(scores, axis=2, keepdims=True))
    probs = (powers / jnp.sum(powers, axis=2, keepdims=True)).astype(BF16)
    attended = jnp.einsum("hqk,khd->qhd", probs, v, preferred_element_type=F32)
    stream = (resid[0].astype(F32) + attended.reshape(tokens, width_all)).astype(BF16)
    wide = lax.optimization_barrier(stream).astype(F32)
    factor = lax.rsqrt(jnp.mean(wide * wide, axis=-1, keepdims=True) + 1e-05)
    normed = (wide * factor * norm_gain).astype(BF16)

    by_expert = expert_gates(expert_ids[0], gate_weights[0], mask_flags[0], experts)
    picked = by_expert != 0.0
    running = jnp.arange(tokens)[:, None] >= jnp.arange(tokens)[None, :]
    rank = jnp.dot(running.astype(BF16), picked.astype(BF16), preferred_element_type=F32) - 1.0
    slot = jnp.arange(capacity, dtype=F32)[None, :, None]
    chosen = jnp.logical_and(rank.T[:, None, :] == slot, picked.T[:, None, :])
    select = chosen.astype(BF16).reshape(experts * capacity, tokens)
    sent_rows = jnp.dot(select, normed, preferred_element_type=F32).astype(BF16)
    gate_rows = jnp.sum(jnp.where(chosen, by_expert.T[:, None, :], 0.0), axis=2).reshape(-1, 1)
    picked_cot = jnp.dot(select, cotangent[0], preferred_element_type=F32)
    sent_grads = (picked_cot * gate_rows).astype(BF16)

    def exchanged(rows):
        rows = rows.reshape(experts, capacity, width_all)
        got = lax.all_to_all(rows, ("ctx", "exp"), split_axis=0, concat_axis=0, tiled=True)
        return got.reshape(-1, width_all)

    input_rows, grad_rows = exchanged(sent_rows), exchanged(sent_grads)
    hidden_width = w_down.shape[2]
    proj = jnp.dot(input_rows, w_gate_up[0], preferred_element_type=F32)
    gate_part, up_part = proj[:, :hidden_width], proj[:, hidden_width:]
    sigma = jax.nn.sigmoid(gate_part)
    activated = gate_part * sigma
    hidden = (activated * up_part).astype(BF16)
    back = jnp.dot(grad_rows, w_down[0], preferred_element_type=F32)
    slope = sigma * (1.0 + gate_part * (1.0 - sigma))
    both = jnp.concatenate([back * up_part * slope, back * activated], axis=1).astype(BF16)
    tn = (((0,), (0,)), ((), ()))
    left = lax.dot_general(input_rows, both, tn, preferred_element_type=F32)
    right = lax.dot_general(grad_rows, hidden, tn, preferred_element_type=F32)
    partial = jnp.concatenate([left, right], axis=1).astype(BF16)
    summed = lax.psum_scatter(partial, "dp", scatter_dimension=0, tiled=True).astype(F32)
    return stream[None], summed[None, :, : 2 * hidden_width], summed[None, :, 2 * hidden_width :]


def solution(mesh):
    rows = P(("dp", "exp"), "ctx", None)
    weights = P(("ctx", "exp"), None, None)
    placed = (rows, rows, rows, rows, P(), rows, rows, P(("dp", "exp"), "ctx"), rows, weights, weights)
    blocks = tuple(mesh.shape[a] for a in ("dp", "ctx", "exp"))
    body = per_device if blocks == (2, 4, 4) else routed_device
    return jax.shard_map(
        body,
        mesh=mesh,
        in_specs=placed,
        out_specs=(rows, P(("ctx", "exp"), "dp", None), P(("ctx", "exp"), "dp", None)),
        check_vma=False,
    )
```

time: 400 us -> 297 us (0.74)
  the two profiles are of different devices: /device:TPU:25 before, /device:TPU:0 now
where the time goes in v2:
time: 297 us; the launch traced here: 293 us
  Pallas kernels  116 us (39%)
  waiting for transfers between devices  62.9 us (21%)
  starting transfers between devices  55.1 us (19%)
  local copies, waits for them, and re-layouts  33.5 us (11%)
  other arithmetic  23.9 us (8%)
    pallas_call x11, Pallas kernels, on_chip(): pl.pallas_call(body, out_shape=shapes, in_specs=[SMEM_SPEC] * scalars + [...  97.6 us
    ppermute x10, waiting for transfers between devices, up(): return lax.ppermute(value, 'ctx', pairs)  52.9 us
    ppermute x28, starting transfers between devices, flipped(): return lax.ppermute(value, axis, [(i, i ^ mask) for i in range(count)])  24.6 us
    ppermute x10, starting transfers between devices, up(): return lax.ppermute(value, 'ctx', pairs)  20.9 us
    pallas_call x2, Pallas kernels, grads(): pl.pallas_call(lambda *refs: grads_kernel(*refs, groups=groups, add=add),...  18.7 us
    ppermute x28, waiting for transfers between devices, flipped(): return lax.ppermute(value, axis, [(i, i ^ mask) for i in range(count)])  10.1 us
    all_to_all x1, starting transfers between devices, per_device(): lax.all_to_all(packed, 'ctx', split_axis=0, concat_axis=0, tiled=True)  9.6 us
    another operation x6, local copies, waits for them, and re-layouts, spread(): over_x = jnp.stack([x0, x1[:count], x2[:count], x3[:count]])  7.89 us
  transfers between devices with their start and end apart: 39, of which 14 were waited for; matrix products, arithmetic and copies ran while one was open for 18% of the time, Pallas kernels for 31%

profile of v2, /device:TPU:0, one launch (start us, length us, event | category | flops | bytes accessed | tf_op | source)
XLA Modules:
  0.0 293.3 jit_solution(12191642564346887206)
XLA Ops:
  3.9 3.0 %pack_heads.1 = bf16[4,4,128,512]{3,2,1,0:T(8,128)(2,1)} custom-call(bf16[128,2048]{1,0:T(8,128)(2,1)} %bitcast.121, bf16[128,2048]{1,0:T(8,128)(2,1)} %bitcast.122, bf16[128,2048]{1,0:T(8,128)(2,1)} %bitcast.123, bf16[128,2048]{1,0:T(8,128)(2,1)} %bitcast.124), custom_call_target="tpu_custom_call" | custom-call | tf_op jit(solution)/shard_map/pack_heads/pallas_call | solution.py:22
  6.8 3.0 %collective-permute-start.11 = (bf16[136,2048]{1,0:T(8,128)(2,1)S(1)}, bf16[136,2048]{1,0:T(8,128)(2,1)S(1)}, u32[]{:S(2)}, u32[]{:S(2)}) collective-permute-start(bf16[136,2048]{1,0:T(8,128)(2,1)S(1)} %pad_maximum_fusion.20), channel_id=1, source_target_pairs={{0,16},{16,0},{1,17},{17,1},{2,18},{18,2},{3,19},{19,3},{4,20},{20... | collective-permute-start | bytes 1671176 | tf_op jit(solution)/shard_map/ppermute | solution.py:242
  9.8 1.5 collective-permute-start.10
  12.6 4.6 %collective-permute-start.8 = (bf16[136,2048]{1,0:T(8,128)(2,1)S(1)}, bf16[136,2048]{1,0:T(8,128)(2,1)S(1)}, u32[]{:S(2)}, u32[]{:S(2)}) collective-permute-start(bf16[136,2048]{1,0:T(8,128)(2,1)S(1)} %pad_maximum_fusion.20), channel_id=1, source_target_pairs={{0,4},{4,8},{8,12},{1,5},{5,9},{9,13},{2,6},{6,10},{10,14},{3,7},{... | collective-permute-start | bytes 1671176 | tf_op jit(solution)/shard_map/ppermute | solution.py:260
  17.2 5.2 %collective-permute-done.11 = bf16[136,2048]{1,0:T(8,128)(2,1)S(1)} collective-permute-done((bf16[136,2048]{1,0:T(8,128)(2,1)S(1)}, bf16[136,2048]{1,0:T(8,128)(2,1)S(1)}, u32[]{:S(2)}, u32[]{:S(2)}) %collective-permute-start.11) | collective-permute-done | bytes 557088 | tf_op jit(solution)/shard_map/ppermute | solution.py:242
  22.4 1.5 collective-permute-done.10
  23.9 3.1 %collective-permute-done.9 = bf16[136,2048]{1,0:T(8,128)(2,1)S(1)} collective-permute-done((bf16[136,2048]{1,0:T(8,128)(2,1)S(1)}, bf16[136,2048]{1,0:T(8,128)(2,1)S(1)}, u32[]{:S(2)}, u32[]{:S(2)}) %collective-permute-start.9) | collective-permute-done | bytes 557088 | tf_op jit(solution)/shard_map/ppermute | solution.py:260
  31.1 1.5 collective-permute-start.12
  33.9 9.6 %all-to-all-start = ((bf16[4,4,128,512]{3,2,1,0:T(8,128)(2,1)}), bf16[4,4,128,512]{3,2,1,0:T(8,128)(2,1)}, u32[]{:S(2)}, u32[]{:S(2)}) async-start(bf16[4,4,128,512]{3,2,1,0:T(8,128)(2,1)} %pack_heads.1), calls=%async_computation | async-start | bytes 4194304 | tf_op jit(solution)/shard_map/all_to_all | solution.py:340
  45.4 2.6 stack.138.place
  48.0 16.9 %collective-permute-done.13 = bf16[136,2048]{1,0:T(8,128)(2,1)} collective-permute-done((bf16[136,2048]{1,0:T(8,128)(2,1)S(1)}, bf16[136,2048]{1,0:T(8,128)(2,1)}, u32[]{:S(2)}, u32[]{:S(2)}) %collective-permute-start.13) | collective-permute-done | bytes 557088 | tf_op jit(solution)/shard_map/ppermute | solution.py:260
  65.9 1.3 select_select_fusion
  67.3 1.6 collective-permute-start.18
  68.9 1.5 collective-permute-start.17
  74.4 1.9 slice_bitcast_fusion.5
  76.3 21.2 %collective-permute-done.16 = bf16[136,2048]{1,0:T(8,128)(2,1)S(1)} collective-permute-done((bf16[136,2048]{1,0:T(8,128)(2,1)S(1)}, bf16[136,2048]{1,0:T(8,128)(2,1)S(1)}, u32[]{:S(2)}, u32[]{:S(2)}) %collective-permute-start.16) | collective-permute-done | bytes 557088 | tf_op jit(solution)/shard_map/ppermute | solution.py:260
  103.3 4.9 %attend.1 = bf16[512,512]{1,0:T(8,128)(2,1)} custom-call(bf16[4,4,128,512]{3,2,1,0:T(8,128)(2,1)} %all-to-all-done.packs), custom_call_target="tpu_custom_call" | custom-call | tf_op jit(solution)/shard_map/attend/pallas_call | solution.py:22
  108.3 2.0 collective-permute-start.3
  110.3 1.5 collective-permute-start.2
  113.1 5.3 %collective-permute-start = (bf16[512,512]{1,0:T(8,128)(2,1)}, bf16[512,512]{1,0:T(8,128)(2,1)}, u32[]{:S(2)}, u32[]{:S(2)}) collective-permute-start(bf16[512,512]{1,0:T(8,128)(2,1)} %attend.1), channel_id=1, source_target_pairs={{0,4},{4,8},{8,12},{1,5},{5,9},{9,13},{2,6},{6,10},{10,14},{3,7},{... | collective-permute-start | bytes 1572872 | tf_op jit(solution)/shard_map/ppermute | solution.py:260
  123.0 1.7 collective-permute-start.29
  124.7 1.5 collective-permute-start.30
  126.2 1.4 collective-permute-done.1
  135.6 1.5 collective-permute-start.4
  140.5 7.5 %cot_rows.4 = (bf16[640,1024]{1,0:T(8,128)(2,1)}, f32[640,512]{1,0:T(8,128)}, f32[640,128]{1,0:T(8,128)}, f32[8,1,128]{2,1,0:T(1,128)}) custom-call(s32[7]{0:T(128)} %stack.138.place, bf16[2048,512]{1,0:T(8,128)(2,1)} %bitcast.103, bf16[4,136,2048]{2,1,0:T(8,128)(2,1)} %copy-done.3, bf16[4,136,2048]{2,1,0:T(8,128)(2,1)} %collective-permute-done.19.refs_1_), custom_call_target="tpu_custom_call" | custom-call | tf_op jit(solution)/shard_map/cot_rows/pallas_call | solution.py:22
  148.1 5.2 %collective-permute-done.5 = bf16[512,512]{1,0:T(8,128)(2,1)S(1)} collective-permute-done((bf16[512,512]{1,0:T(8,128)(2,1)}, bf16[512,512]{1,0:T(8,128)(2,1)S(1)}, u32[]{:S(2)}, u32[]{:S(2)}) %collective-permute-start.5) | collective-permute-done | bytes 524320 | tf_op jit(solution)/shard_map/ppermute | solution.py:260
  155.5 2.1 select_select_fusion.1
  158.9 1.4 collective-permute-start.22
  160.3 1.5 collective-permute-start.21
  162.2 1.5 collective-permute-start.20
  164.7 1.9 slice_bitcast_fusion.11
  166.5 1.9 slice_bitcast_fusion.8
  168.4 7.6 %cot_rows.5 = (bf16[640,1024]{1,0:T(8,128)(2,1)}, f32[640,512]{1,0:T(8,128)}, f32[640,128]{1,0:T(8,128)}, f32[8,1,128]{2,1,0:T(1,128)}) custom-call(s32[7]{0:T(128)} %stack.138.place, bf16[2048,512]{1,0:T(8,128)(2,1)} %bitcast.104, bf16[4,136,2048]{2,1,0:T(8,128)(2,1)} %copy-done.1, bf16[4,136,2048]{2,1,0:T(8,128)(2,1)} %collective-permute-done.25.refs_1_), custom_call_target="tpu_custom_call" | custom-call | tf_op jit(solution)/shard_map/cot_rows/pallas_call | solution.py:22
  176.0 2.7 collective-permute-done.20
  183.6 1.5 slice_bitcast_fusion.10
  185.2 7.6 %cot_rows.6 = (bf16[640,1024]{1,0:T(8,128)(2,1)}, f32[640,512]{1,0:T(8,128)}, f32[640,128]{1,0:T(8,128)}, f32[8,1,128]{2,1,0:T(1,128)}) custom-call(s32[7]{0:T(128)} %stack.138.place, bf16[2048,512]{1,0:T(8,128)(2,1)} %bitcast.105, bf16[4,136,2048]{2,1,0:T(8,128)(2,1)} %copy-done.2, bf16[4,136,2048]{2,1,0:T(8,128)(2,1)} %collective-permute-done.26.refs_1_), custom_call_target="tpu_custom_call" | custom-call | tf_op jit(solution)/shard_map/cot_rows/pallas_call | solution.py:22
  193.9 7.6 %cot_rows.7 = (bf16[640,1024]{1,0:T(8,128)(2,1)}, f32[640,512]{1,0:T(8,128)}, f32[640,128]{1,0:T(8,128)}, f32[8,1,128]{2,1,0:T(1,128)}) custom-call(s32[7]{0:T(128)} %stack.138.place, bf16[2048,512]{1,0:T(8,128)(2,1)} %bitcast.106, bf16[4,136,2048]{2,1,0:T(8,128)(2,1)} %copy-done.4, bf16[4,136,2048]{2,1,0:T(8,128)(2,1)} %collective-permute-done.31.refs_1_), custom_call_target="tpu_custom_call" | custom-call | tf_op jit(solution)/shard_map/cot_rows/pallas_call | solution.py:22
  205.1 1.6 collective-permute-start.33
  207.8 1.6 pad_maximum_fusion.7.refs_0_
  211.4 1.8 collective-permute-done.33
  213.6 23.8 %stream_rows.5 = (bf16[640,1024]{1,0:T(8,128)(2,1)}, bf16[640,1024]{1,0:T(8,128)(2,1)}, bf16[640,512]{1,0:T(8,128)(2,1)}) custom-call(s32[7]{0:T(128)} %stack.138.place, f32[4,1,512]{2,1,0:T(1,128)} %bitcast.125, bf16[2048,1024]{1,0:T(8,128)(2,1)} %bitcast.99, f32[640,512]{1,0:T(8,128)} %get-tuple-element.78.back_in, f32[640,128]{1,0:T(8,128)} %get-tuple-element.79.columns, ...), custom_call_target="tpu_custom_call" | custom-call | tf_op jit(solution)/shard_map/stream_rows/pallas_call | solution.py:22
  237.4 2.5 own_rows.1
  239.9 11.1 %stream_rows.7 = (bf16[640,1024]{1,0:T(8,128)(2,1)}, bf16[640,1024]{1,0:T(8,128)(2,1)}, bf16[640,512]{1,0:T(8,128)(2,1)}) custom-call(s32[7]{0:T(128)} %stack.138.place, f32[4,1,512]{2,1,0:T(1,128)} %bitcast.126, bf16[2048,1024]{1,0:T(8,128)(2,1)} %bitcast.100, f32[640,512]{1,0:T(8,128)} %get-tuple-element.89.back_in, f32[640,128]{1,0:T(8,128)} %get-tuple-element.90.columns, ...), custom_call_target="tpu_custom_call" | custom-call | tf_op jit(solution)/shard_map/stream_rows/pallas_call | solution.py:22
  250.9 8.6 %grads.2 = (f32[1,1024,1024]{2,1,0:T(8,128)}, f32[1,1024,512]{2,1,0:T(8,128)}) custom-call(bf16[640,1024]{1,0:T(8,128)(2,1)} %get-tuple-element.107.refs_0_, bf16[640,1024]{1,0:T(8,128)(2,1)} %get-tuple-element.116.refs_1_, bf16[640,1024]{1,0:T(8,128)(2,1)} %get-tuple-element.77.refs_2_, bf16[640,1024]{1,0:T(8,128)(2,1)} %get-tuple-element.88.refs_3_, ...), custom_call_target="tpu_custom_call" | custom-call | tf_op jit(solution)/shard_map/grads/pallas_call | solution.py:225
  259.6 11.0 %stream_rows.4 = (bf16[640,1024]{1,0:T(8,128)(2,1)}, bf16[640,1024]{1,0:T(8,128)(2,1)}, bf16[640,512]{1,0:T(8,128)(2,1)}) custom-call(s32[7]{0:T(128)} %stack.138.place, f32[4,1,512]{2,1,0:T(1,128)} %bitcast.127, bf16[2048,1024]{1,0:T(8,128)(2,1)} %bitcast.101, f32[640,512]{1,0:T(8,128)} %get-tuple-element.94.back_in, f32[640,128]{1,0:T(8,128)} %get-tuple-element.95.columns, ...), custom_call_target="tpu_custom_call" | custom-call | tf_op jit(solution)/shard_map/stream_rows/pallas_call | solution.py:22
  270.6 1.4 copy-done.17
  272.0 11.1 %stream_rows.6 = (bf16[640,1024]{1,0:T(8,128)(2,1)}, bf16[640,1024]{1,0:T(8,128)(2,1)}, bf16[640,512]{1,0:T(8,128)(2,1)}) custom-call(s32[7]{0:T(128)} %stack.138.place, f32[4,1,512]{2,1,0:T(1,128)} %bitcast.128, bf16[2048,1024]{1,0:T(8,128)(2,1)} %bitcast.102, f32[640,512]{1,0:T(8,128)} %get-tuple-element.101.back_in, ...), custom_call_target="tpu_custom_call" | custom-call | tf_op jit(solution)/shard_map/stream_rows/pallas_call | solution.py:22
  283.1 10.1 %grads.3 = (f32[1,1024,1024]{2,1,0:T(8,128)}, f32[1,1024,512]{2,1,0:T(8,128)}) custom-call(bf16[640,1024]{1,0:T(8,128)(2,1)} %get-tuple-element.105.refs_0_, bf16[640,1024]{1,0:T(8,128)(2,1)} %get-tuple-element.111.refs_1_, bf16[640,1024]{1,0:T(8,128)(2,1)} %get-tuple-element.99.refs_2_, ...), custom_call_target="tpu_custom_call", output_to_operand_aliasing={{0}: (8, {}), {1}: (9, {})} | custom-call | tf_op jit(solution)/shard_map/grads/pallas_call | solution.py:225
  (188 shorter events, 57.6 us)
Async XLA Ops:
  6.8 15.6 %collective-permute-start.11 = (bf16[136,2048]{1,0:T(8,128)(2,1)S(1)}, bf16[136,2048]{1,0:T(8,128)(2,1)S(1)}, u32[]{:S(2)}, u32[]{:S(2)}) collective-permute-start(bf16[136,2048]{1,0:T(8,128)(2,1)S(1)} %pad_maximum_fusion.20), channel_id=1, source_target_pairs={{0,16},{16,0},{1,17},{17,1},{2,18},{18,2},{3,19},{19,3},{4,20},{20... | collective-permute-start | bytes 1671176 | tf_op jit(solution)/shard_map/ppermute | solution.py:242
  9.8 14.1 %collective-permute-start.10 = (bf16[136,2048]{1,0:T(8,128)(2,1)S(1)}, bf16[136,2048]{1,0:T(8,128)(2,1)S(1)}, u32[]{:S(2)}, u32[]{:S(2)}) collective-permute-start(bf16[136,2048]{1,0:T(8,128)(2,1)S(1)} %pad_maximum_fusion.20), channel_id=1, source_target_pairs={{0,2},{1,3},{2,0},{3,1},{4,6},{5,7},{6,4},{7,5},{8,10},{9,11},{10,... | collective-permute-start | bytes 1671176 | tf_op jit(solution)/shard_map/ppermute | solution.py:242
  11.3 15.7 %collective-permute-start.9 = (bf16[136,2048]{1,0:T(8,128)(2,1)S(1)}, bf16[136,2048]{1,0:T(8,128)(2,1)S(1)}, u32[]{:S(2)}, u32[]{:S(2)}) collective-permute-start(bf16[136,2048]{1,0:T(8,128)(2,1)S(1)} %pad_maximum_fusion.20), channel_id=1, source_target_pairs={{4,0},{8,4},{12,8},{5,1},{9,5},{13,9},{6,2},{10,6},{14,10},{7,3},{... | collective-permute-start | bytes 1671176 | tf_op jit(solution)/shard_map/ppermute | solution.py:260
  12.6 15.6 %collective-permute-start.8 = (bf16[136,2048]{1,0:T(8,128)(2,1)S(1)}, bf16[136,2048]{1,0:T(8,128)(2,1)S(1)}, u32[]{:S(2)}, u32[]{:S(2)}) collective-permute-start(bf16[136,2048]{1,0:T(8,128)(2,1)S(1)} %pad_maximum_fusion.20), channel_id=1, source_target_pairs={{0,4},{4,8},{8,12},{1,5},{5,9},{9,13},{2,6},{6,10},{10,14},{3,7},{... | collective-permute-start | bytes 1671176 | tf_op jit(solution)/shard_map/ppermute | solution.py:260
  29.3 35.6 %collective-permute-start.14 = (bf16[208,2048]{1,0:T(8,128)(2,1)}, bf16[208,2048]{1,0:T(8,128)(2,1)}, u32[]{:S(2)}, u32[]{:S(2)}) collective-permute-start(bf16[208,2048]{1,0:T(8,128)(2,1)} %pad_maximum_fusion.8), channel_id=1, source_target_pairs={{0,2},{1,3},{2,0},{3,1},{4,6},{5,7},{6,4},{7,5},{8,10},{9,11},{10,... | collective-permute-start | bytes 2555912 | tf_op jit(solution)/shard_map/ppermute | solution.py:242
  30.8 12.7 %copy-start.33 = (s32[4]{0:T(128)S(1)}, s32[4]{0:T(128)}, u32[]{:S(2)}) copy-start(s32[4]{0:T(128)} %constant.35.clone) | copy-start | bytes 52
  30.8 13.3 %copy-start.32 = (s32[4]{0:T(128)S(1)}, s32[4]{0:T(128)}, u32[]{:S(2)}) copy-start(s32[4]{0:T(128)} %constant.34.clone) | copy-start | bytes 52
  30.8 14.0 %copy-start.31 = (s32[4]{0:T(128)S(1)}, s32[4]{0:T(128)}, u32[]{:S(2)}) copy-start(s32[4]{0:T(128)} %constant.33.clone) | copy-start | bytes 52
  30.8 34.1 %collective-permute-start.15 = (bf16[200,2048]{1,0:T(8,128)(2,1)}, bf16[200,2048]{1,0:T(8,128)(2,1)S(1)}, u32[]{:S(2)}, u32[]{:S(2)}) collective-permute-start(bf16[200,2048]{1,0:T(8,128)(2,1)} %pad_maximum_fusion.17), channel_id=1, source_target_pairs={{0,16},{16,0},{1,17},{17,1},{2,18},{18,2},{3,19},{19,3},{4,20},{20... | collective-permute-start | bytes 2457608 | tf_op jit(solution)/shard_map/ppermute | solution.py:242
  31.1 16.8 %collective-permute-start.12 = (bf16[136,2048]{1,0:T(8,128)(2,1)}, bf16[136,2048]{1,0:T(8,128)(2,1)}, u32[]{:S(2)}, u32[]{:S(2)}) collective-permute-start(bf16[136,2048]{1,0:T(8,128)(2,1)} %copy-done.30), channel_id=1, source_target_pairs={{4,8},{8,12},{5,9},{9,13},{6,10},{10,14},{7,11},{11,15},{20,24},{2... | collective-permute-start | bytes 1671176 | tf_op jit(solution)/shard_map/ppermute | solution.py:260
  32.6 32.2 %collective-permute-start.13 = (bf16[136,2048]{1,0:T(8,128)(2,1)S(1)}, bf16[136,2048]{1,0:T(8,128)(2,1)}, u32[]{:S(2)}, u32[]{:S(2)}) collective-permute-start(bf16[136,2048]{1,0:T(8,128)(2,1)S(1)} %collective-permute-done.9), channel_id=1, source_target_pairs={{4,0},{8,4},{5,1},{9,5},{6,2},{10,6},{7,3},{11,7},{20,16},{24,20},... | collective-permute-start | bytes 1671176 | tf_op jit(solution)/shard_map/ppermute | solution.py:260
  33.9 69.4 %all-to-all-start = ((bf16[4,4,128,512]{3,2,1,0:T(8,128)(2,1)}), bf16[4,4,128,512]{3,2,1,0:T(8,128)(2,1)}, u32[]{:S(2)}, u32[]{:S(2)}) async-start(bf16[4,4,128,512]{3,2,1,0:T(8,128)(2,1)} %pack_heads.1), calls=%async_computation | async-start | bytes 4194304 | tf_op jit(solution)/shard_map/all_to_all | solution.py:340
  67.3 30.2 %collective-permute-start.18 = (bf16[200,2048]{1,0:T(8,128)(2,1)S(1)}, bf16[200,2048]{1,0:T(8,128)(2,1)S(1)}, u32[]{:S(2)}, u32[]{:S(2)}) collective-permute-start(bf16[200,2048]{1,0:T(8,128)(2,1)S(1)} %pad_maximum_fusion.18), channel_id=1, source_target_pairs={{0,16},{16,0},{1,17},{17,1},{2,18},{18,2},{3,19},{19,3},{4,20},{20... | collective-permute-start | bytes 2457608 | tf_op jit(solution)/shard_map/ppermute | solution.py:242
  68.9 28.6 %collective-permute-start.17 = (bf16[208,2048]{1,0:T(8,128)(2,1)S(1)}, bf16[208,2048]{1,0:T(8,128)(2,1)S(1)}, u32[]{:S(2)}, u32[]{:S(2)}) collective-permute-start(bf16[208,2048]{1,0:T(8,128)(2,1)S(1)} %pad_maximum_fusion.9), channel_id=1, source_target_pairs={{0,2},{1,3},{2,0},{3,1},{4,6},{5,7},{6,4},{7,5},{8,10},{9,11},{10,... | collective-permute-start | bytes 2555912 | tf_op jit(solution)/shard_map/ppermute | solution.py:242
  72.3 25.2 %collective-permute-start.16 = (bf16[136,2048]{1,0:T(8,128)(2,1)S(1)}, bf16[136,2048]{1,0:T(8,128)(2,1)S(1)}, u32[]{:S(2)}, u32[]{:S(2)}) collective-permute-start(bf16[136,2048]{1,0:T(8,128)(2,1)S(1)} %get-tuple-element.124), channel_id=1, source_target_pairs={{4,0},{8,12},{5,1},{9,13},{6,2},{10,14},{7,3},{11,15},{20,16},{24,... | collective-permute-start | bytes 1671176 | tf_op jit(solution)/shard_map/ppermute | solution.py:260
  98.6 13.2 %collective-permute-start.24 = (bf16[200,2048]{1,0:T(8,128)(2,1)}, bf16[200,2048]{1,0:T(8,128)(2,1)}, u32[]{:S(2)}, u32[]{:S(2)}) collective-permute-start(bf16[200,2048]{1,0:T(8,128)(2,1)} %pad_maximum_fusion.19), channel_id=1, source_target_pairs={{0,16},{16,0},{1,17},{17,1},{2,18},{18,2},{3,19},{19,3},{4,20},{20... | collective-permute-start | bytes 2457608 | tf_op jit(solution)/shard_map/ppermute | solution.py:242
  100.1 13.0 %collective-permute-start.23 = (bf16[208,2048]{1,0:T(8,128)(2,1)}, bf16[208,2048]{1,0:T(8,128)(2,1)}, u32[]{:S(2)}, u32[]{:S(2)}) collective-permute-start(bf16[208,2048]{1,0:T(8,128)(2,1)} %pad_maximum_fusion.10), channel_id=1, source_target_pairs={{0,2},{1,3},{2,0},{3,1},{4,6},{5,7},{6,4},{7,5},{8,10},{9,11},{10,... | collective-permute-start | bytes 2555912 | tf_op jit(solution)/shard_map/ppermute | solution.py:242
  101.3 35.7 %collective-permute-start.19 = (bf16[4,136,2048]{2,1,0:T(8,128)(2,1)S(1)}, bf16[4,136,2048]{2,1,0:T(8,128)(2,1)}, u32[]{:S(2)}, u32[]{:S(2)}) collective-permute-start(bf16[4,136,2048]{2,1,0:T(8,128)(2,1)S(1)} %pad_maximum_fusion.refs_0_), channel_id=1, source_target_pairs={{0,1},{1,0},{2,3},{3,2},{4,5},{5,4},{6,7},{7,6},{8,9},{9,8},{10,11... | collective-permute-start | bytes 6684680 | tf_op jit(solution)/shard_map/ppermute | solution.py:242
  103.3 18.2 %copy-start.13 = (bf16[1,136,2048]{2,1,0:T(8,128)(2,1)S(1)}, bf16[1,136,2048]{2,1,0:T(8,128)(2,1)}, u32[]{:S(2)}) copy-start(bf16[1,136,2048]{2,1,0:T(8,128)(2,1)} %slice_bitcast_fusion.5) | copy-start | bytes 1671172
  103.3 18.2 %copy-start.16 = (bf16[1,136,2048]{2,1,0:T(8,128)(2,1)S(1)}, bf16[1,136,2048]{2,1,0:T(8,128)(2,1)}, u32[]{:S(2)}) copy-start(bf16[1,136,2048]{2,1,0:T(8,128)(2,1)} %slice_bitcast_fusion.4) | copy-start | bytes 1671172
  103.3 18.2 %copy-start.25 = (bf16[136,2048]{1,0:T(8,128)(2,1)S(1)}, bf16[136,2048]{1,0:T(8,128)(2,1)}, u32[]{:S(2)}) copy-start(bf16[136,2048]{1,0:T(8,128)(2,1)} %copy-done.24) | copy-start | bytes 1671172
  108.3 14.7 %collective-permute-start.3 = (bf16[512,512]{1,0:T(8,128)(2,1)}, bf16[512,512]{1,0:T(8,128)(2,1)S(1)}, u32[]{:S(2)}, u32[]{:S(2)}) collective-permute-start(bf16[512,512]{1,0:T(8,128)(2,1)} %attend.1), channel_id=1, source_target_pairs={{0,16},{16,0},{1,17},{17,1},{2,18},{18,2},{3,19},{19,3},{4,20},{20... | collective-permute-start | bytes 1572872 | tf_op jit(solution)/shard_map/ppermute | solution.py:242
  110.3 14.4 %collective-permute-start.2 = (bf16[512,512]{1,0:T(8,128)(2,1)}, bf16[512,512]{1,0:T(8,128)(2,1)S(1)}, u32[]{:S(2)}, u32[]{:S(2)}) collective-permute-start(bf16[512,512]{1,0:T(8,128)(2,1)} %attend.1), channel_id=1, source_target_pairs={{0,2},{1,3},{2,0},{3,1},{4,6},{5,7},{6,4},{7,5},{8,10},{9,11},{10,... | collective-permute-start | bytes 1572872 | tf_op jit(solution)/shard_map/ppermute | solution.py:242
  111.8 15.8 %collective-permute-start.1 = (bf16[512,512]{1,0:T(8,128)(2,1)}, bf16[512,512]{1,0:T(8,128)(2,1)}, u32[]{:S(2)}, u32[]{:S(2)}) collective-permute-start(bf16[512,512]{1,0:T(8,128)(2,1)} %attend.1), channel_id=1, source_target_pairs={{4,0},{8,4},{12,8},{5,1},{9,5},{13,9},{6,2},{10,6},{14,10},{7,3},{... | collective-permute-start | bytes 1572872 | tf_op jit(solution)/shard_map/ppermute | solution.py:260
  113.1 15.7 %collective-permute-start = (bf16[512,512]{1,0:T(8,128)(2,1)}, bf16[512,512]{1,0:T(8,128)(2,1)}, u32[]{:S(2)}, u32[]{:S(2)}) collective-permute-start(bf16[512,512]{1,0:T(8,128)(2,1)} %attend.1), channel_id=1, source_target_pairs={{0,4},{4,8},{8,12},{1,5},{5,9},{9,13},{2,6},{6,10},{10,14},{3,7},{... | collective-permute-start | bytes 1572872 | tf_op jit(solution)/shard_map/ppermute | solution.py:260
  121.8 9.4 %copy-start.1 = (bf16[4,136,2048]{2,1,0:T(8,128)(2,1)}, bf16[4,136,2048]{2,1,0:T(8,128)(2,1)S(1)}, u32[]{:S(2)}) copy-start(bf16[4,136,2048]{2,1,0:T(8,128)(2,1)S(1)} %pad_maximum_fusion.1.refs_0_) | copy-start | bytes 6684676
  123.0 8.9 %collective-permute-start.29 = (bf16[64,2048]{1,0:T(8,128)(2,1)S(1)}, bf16[64,2048]{1,0:T(8,128)(2,1)S(1)}, u32[]{:S(2)}, u32[]{:S(2)}) collective-permute-start(bf16[64,2048]{1,0:T(8,128)(2,1)S(1)} %slice.146), channel_id=1, source_target_pairs={{0,16},{16,0},{1,17},{17,1},{2,18},{18,2},{3,19},{19,3},{4,20},{20... | collective-permute-start | bytes 786440 | tf_op jit(solution)/shard_map/ppermute | solution.py:242
  124.7 10.9 %collective-permute-start.30 = (bf16[72,2048]{1,0:T(8,128)(2,1)S(1)}, bf16[72,2048]{1,0:T(8,128)(2,1)S(1)}, u32[]{:S(2)}, u32[]{:S(2)}) collective-permute-start(bf16[72,2048]{1,0:T(8,128)(2,1)S(1)} %slice.147), channel_id=1, source_target_pairs={{0,2},{1,3},{2,0},{3,1},{4,6},{5,7},{6,4},{7,5},{8,10},{9,11},{10,... | collective-permute-start | bytes 884744 | tf_op jit(solution)/shard_map/ppermute | solution.py:242
  127.6 34.6 %collective-permute-start.25 = (bf16[4,136,2048]{2,1,0:T(8,128)(2,1)S(1)}, bf16[4,136,2048]{2,1,0:T(8,128)(2,1)}, u32[]{:S(2)}, u32[]{:S(2)}) collective-permute-start(bf16[4,136,2048]{2,1,0:T(8,128)(2,1)S(1)} %pad_maximum_fusion.1.refs_0_), channel_id=1, source_target_pairs={{0,1},{1,0},{2,3},{3,2},{4,5},{5,4},{6,7},{7,6},{8,9},{9,8},{10,11... | collective-permute-start | bytes 6684680 | tf_op jit(solution)/shard_map/ppermute | solution.py:242
  131.3 22.0 %collective-permute-start.7 = (bf16[768,512]{1,0:T(8,128)(2,1)}, bf16[768,512]{1,0:T(8,128)(2,1)}, u32[]{:S(2)}, u32[]{:S(2)}) collective-permute-start(bf16[768,512]{1,0:T(8,128)(2,1)} %get-tuple-element.143), channel_id=1, source_target_pairs={{0,16},{16,0},{1,17},{17,1},{2,18},{18,2},{3,19},{19,3},{4,20},{20... | collective-permute-start | bytes 2359304 | tf_op jit(solution)/shard_map/ppermute | solution.py:242
  131.9 21.4 %collective-permute-start.6 = (bf16[768,512]{1,0:T(8,128)(2,1)}, bf16[768,512]{1,0:T(8,128)(2,1)}, u32[]{:S(2)}, u32[]{:S(2)}) collective-permute-start(bf16[768,512]{1,0:T(8,128)(2,1)} %get-tuple-element.144), channel_id=1, source_target_pairs={{0,2},{1,3},{2,0},{3,1},{4,6},{5,7},{6,4},{7,5},{8,10},{9,11},{10,... | collective-permute-start | bytes 2359304 | tf_op jit(solution)/shard_map/ppermute | solution.py:242
  135.6 12.4 %collective-permute-start.4 = (bf16[512,512]{1,0:T(8,128)(2,1)}, bf16[512,512]{1,0:T(8,128)(2,1)}, u32[]{:S(2)}, u32[]{:S(2)}) collective-permute-start(bf16[512,512]{1,0:T(8,128)(2,1)} %collective-permute-done), channel_id=1, source_target_pairs={{4,8},{8,12},{5,9},{9,13},{6,10},{10,14},{7,11},{11,15},{20,24},{2... | collective-permute-start | bytes 1572872 | tf_op jit(solution)/shard_map/ppermute | solution.py:260
  137.1 16.2 %collective-permute-start.5 = (bf16[512,512]{1,0:T(8,128)(2,1)}, bf16[512,512]{1,0:T(8,128)(2,1)S(1)}, u32[]{:S(2)}, u32[]{:S(2)}) collective-permute-start(bf16[512,512]{1,0:T(8,128)(2,1)} %collective-permute-done.1), channel_id=1, source_target_pairs={{4,0},{8,4},{5,1},{9,5},{6,2},{10,6},{7,3},{11,7},{20,16},{24,20},... | collective-permute-start | bytes 1572872 | tf_op jit(solution)/shard_map/ppermute | solution.py:260
  148.0 37.2 %collective-permute-start.26 = (bf16[4,136,2048]{2,1,0:T(8,128)(2,1)S(1)}, bf16[4,136,2048]{2,1,0:T(8,128)(2,1)}, u32[]{:S(2)}, u32[]{:S(2)}) collective-permute-start(bf16[4,136,2048]{2,1,0:T(8,128)(2,1)S(1)} %pad_maximum_fusion.2.refs_0_), channel_id=1, source_target_pairs={{0,1},{1,0},{2,3},{3,2},{4,5},{5,4},{6,7},{7,6},{8,9},{9,8},{10,11... | collective-permute-start | bytes 6684680 | tf_op jit(solution)/shard_map/ppermute | solution.py:242
  158.9 19.7 %collective-permute-start.22 = (bf16[768,512]{1,0:T(8,128)(2,1)}, bf16[768,512]{1,0:T(8,128)(2,1)}, u32[]{:S(2)}, u32[]{:S(2)}) collective-permute-start(bf16[768,512]{1,0:T(8,128)(2,1)} %get-tuple-element.141), channel_id=1, source_target_pairs={{0,16},{16,0},{1,17},{17,1},{2,18},{18,2},{3,19},{19,3},{4,20},{20... | collective-permute-start | bytes 2359304 | tf_op jit(solution)/shard_map/ppermute | solution.py:242
  160.3 18.3 %collective-permute-start.21 = (bf16[768,512]{1,0:T(8,128)(2,1)}, bf16[768,512]{1,0:T(8,128)(2,1)}, u32[]{:S(2)}, u32[]{:S(2)}) collective-permute-start(bf16[768,512]{1,0:T(8,128)(2,1)} %get-tuple-element.142), channel_id=1, source_target_pairs={{0,2},{1,3},{2,0},{3,1},{4,6},{5,7},{6,4},{7,5},{8,10},{9,11},{10,... | collective-permute-start | bytes 2359304 | tf_op jit(solution)/shard_map/ppermute | solution.py:242
  162.1 13.8 %copy-start.4 = (bf16[4,136,2048]{2,1,0:T(8,128)(2,1)}, bf16[4,136,2048]{2,1,0:T(8,128)(2,1)S(1)}, u32[]{:S(2)}) copy-start(bf16[4,136,2048]{2,1,0:T(8,128)(2,1)S(1)} %pad_maximum_fusion.3.refs_0_) | copy-start | bytes 6684676
  162.1 31.7 %collective-permute-start.31 = (bf16[4,136,2048]{2,1,0:T(8,128)(2,1)S(1)}, bf16[4,136,2048]{2,1,0:T(8,128)(2,1)}, u32[]{:S(2)}, u32[]{:S(2)}) collective-permute-start(bf16[4,136,2048]{2,1,0:T(8,128)(2,1)S(1)} %pad_maximum_fusion.3.refs_0_), channel_id=1, source_target_pairs={{0,1},{1,0},{2,3},{3,2},{4,5},{5,4},{6,7},{7,6},{8,9},{9,8},{10,11... | collective-permute-start | bytes 6684680 | tf_op jit(solution)/shard_map/ppermute | solution.py:242
  162.2 16.4 %collective-permute-start.20 = (bf16[512,512]{1,0:T(8,128)(2,1)}, bf16[512,512]{1,0:T(8,128)(2,1)S(1)}, u32[]{:S(2)}, u32[]{:S(2)}) collective-permute-start(bf16[512,512]{1,0:T(8,128)(2,1)} %get-tuple-element.126), channel_id=1, source_target_pairs={{4,0},{8,12},{5,1},{9,13},{6,2},{10,14},{7,3},{11,15},{20,16},{24,... | collective-permute-start | bytes 1572872 | tf_op jit(solution)/shard_map/ppermute | solution.py:260
  182.1 19.5 %collective-permute-start.28 = (bf16[768,512]{1,0:T(8,128)(2,1)}, bf16[768,512]{1,0:T(8,128)(2,1)}, u32[]{:S(2)}, u32[]{:S(2)}) collective-permute-start(bf16[768,512]{1,0:T(8,128)(2,1)} %get-tuple-element.139), channel_id=1, source_target_pairs={{0,16},{16,0},{1,17},{17,1},{2,18},{18,2},{3,19},{19,3},{4,20},{20... | collective-permute-start | bytes 2359304 | tf_op jit(solution)/shard_map/ppermute | solution.py:242
  182.6 19.2 %collective-permute-start.27 = (bf16[768,512]{1,0:T(8,128)(2,1)}, bf16[768,512]{1,0:T(8,128)(2,1)}, u32[]{:S(2)}, u32[]{:S(2)}) collective-permute-start(bf16[768,512]{1,0:T(8,128)(2,1)} %get-tuple-element.140), channel_id=1, source_target_pairs={{0,2},{1,3},{2,0},{3,1},{4,6},{5,7},{6,4},{7,5},{8,10},{9,11},{10,... | collective-permute-start | bytes 2359304 | tf_op jit(solution)/shard_map/ppermute | solution.py:242
  183.5 30.0 %collective-permute-start.35 = (bf16[4,512,512]{2,1,0:T(8,128)(2,1)S(1)}, bf16[4,512,512]{2,1,0:T(8,128)(2,1)}, u32[]{:S(2)}, u32[]{:S(2)}) collective-permute-start(bf16[4,512,512]{2,1,0:T(8,128)(2,1)S(1)} %pad_maximum_fusion.4.slices.refs_0_), channel_id=1, source_target_pairs={{0,1},{1,0},{2,3},{3,2},{4,5},{5,4},{6,7},{7,6},{8,9},{9,8},{10,11... | collective-permute-start | bytes 6291464 | tf_op jit(solution)/shard_map/ppermute | solution.py:242
  202.9 8.5 %collective-permute-start.34 = (bf16[256,512]{1,0:T(8,128)(2,1)S(1)}, bf16[256,512]{1,0:T(8,128)(2,1)S(1)}, u32[]{:S(2)}, u32[]{:S(2)}) collective-permute-start(bf16[256,512]{1,0:T(8,128)(2,1)S(1)} %get-tuple-element.136), channel_id=1, source_target_pairs={{0,2},{1,3},{2,0},{3,1},{4,6},{5,7},{6,4},{7,5},{8,10},{9,11},{10,... | collective-permute-start | bytes 786440 | tf_op jit(solution)/shard_map/ppermute | solution.py:242
  205.1 8.1 %collective-permute-start.33 = (bf16[256,512]{1,0:T(8,128)(2,1)S(1)}, bf16[256,512]{1,0:T(8,128)(2,1)S(1)}, u32[]{:S(2)}, u32[]{:S(2)}) collective-permute-start(bf16[256,512]{1,0:T(8,128)(2,1)S(1)} %get-tuple-element.138), channel_id=1, source_target_pairs={{0,16},{16,0},{1,17},{17,1},{2,18},{18,2},{3,19},{19,3},{4,20},{20... | collective-permute-start | bytes 786440 | tf_op jit(solution)/shard_map/ppermute | solution.py:242
  209.4 30.4 %collective-permute-start.37 = (bf16[4,512,512]{2,1,0:T(8,128)(2,1)}, bf16[4,512,512]{2,1,0:T(8,128)(2,1)}, u32[]{:S(2)}, u32[]{:S(2)}) collective-permute-start(bf16[4,512,512]{2,1,0:T(8,128)(2,1)} %pad_maximum_fusion.7.refs_0_), channel_id=1, source_target_pairs={{0,1},{1,0},{2,3},{3,2},{4,5},{5,4},{6,7},{7,6},{8,9},{9,8},{10,11... | collective-permute-start | bytes 6291464 | tf_op jit(solution)/shard_map/ppermute | solution.py:242
  210.8 48.8 %collective-permute-start.32 = (bf16[4,512,512]{2,1,0:T(8,128)(2,1)S(1)}, bf16[4,512,512]{2,1,0:T(8,128)(2,1)}, u32[]{:S(2)}, u32[]{:S(2)}) collective-permute-start(bf16[4,512,512]{2,1,0:T(8,128)(2,1)S(1)} %pad_maximum_fusion.5.refs_0_), channel_id=1, source_target_pairs={{0,1},{1,0},{2,3},{3,2},{4,5},{5,4},{6,7},{7,6},{8,9},{9,8},{10,11... | collective-permute-start | bytes 6291464 | tf_op jit(solution)/shard_map/ppermute | solution.py:242
  213.6 23.8 %copy-start.6 = (bf16[4,512,512]{2,1,0:T(8,128)(2,1)}, bf16[4,512,512]{2,1,0:T(8,128)(2,1)S(1)}, u32[]{:S(2)}) copy-start(bf16[4,512,512]{2,1,0:T(8,128)(2,1)S(1)} %pad_maximum_fusion.6.refs_0_) | copy-start | bytes 6291460
  237.4 33.3 %collective-permute-start.36 = (bf16[4,512,512]{2,1,0:T(8,128)(2,1)S(1)}, bf16[4,512,512]{2,1,0:T(8,128)(2,1)S(1)}, u32[]{:S(2)}, u32[]{:S(2)}) collective-permute-start(bf16[4,512,512]{2,1,0:T(8,128)(2,1)S(1)} %pad_maximum_fusion.6.refs_0_), channel_id=1, source_target_pairs={{0,1},{1,0},{2,3},{3,2},{4,5},{5,4},{6,7},{7,6},{8,9},{9,8},{10,11... | collective-permute-start | bytes 6291464 | tf_op jit(solution)/shard_map/ppermute | solution.py:242
  (25 other events, 134.2 us)
